TPU v7x, 256 devices: a whole 4x4x8 slice. The times are simulated.
256 devices in a mesh: expert: 64 (over z_hi, y, x, core), hidden: 4 (over z_lo).
Axes of the slice: x: 4, y: 4, z: 8 (z_hi: 2, z_lo: 4; z = z_hi * 4 + z_lo), core: 2. Of those that a mesh axis runs over, the one named last changes fastest.
Arguments:
- cotangent: bfloat16 [65536, 2048], P(('expert', 'hidden')), may hold values from -6 to 6
- slot_token: int32 [256, 64, 10], P(('expert', 'hidden')), may hold values from -1 to 255, as said below
- slot_gate: float32 [256, 64, 10], P(('expert', 'hidden')), may hold values from 0.1 to 1
- w_down: bfloat16 [64, 4096, 2048], P('expert', 'hidden'), may hold values from -0.09375 to 0.09375
Outputs:
- hidden_grad: bfloat16 [64, 2048, 4096], P('expert', None, 'hidden')
Inputs may be any that keep to these rules, and one draw needn't show every extreme that they name: `slot_token`: on each device and for each expert the live slots come first and name distinct local tokens; a device fills at most 10 slots for one expert. For each expert and each index of the hidden axis, the 64 devices with that index name exactly 512 tokens together, so each expert takes exactly 2048 tokens.
All inputs are finite; a program needn't handle non-finite values.
Results may differ from a plain program's by a relative error of at most 0.0049.
Values may be sent and summed in bfloat16 or wider, within the bound.
No kernel may reach another device: no remote copies, remote signals or barrier semaphores. Data moves between devices by JAX's collectives and lax.ppermute only.
A program may use at most 128 MiB of HBM per device.

v0:
```python
import jax
import jax.numpy as jnp
from jax import lax
from jax.sharding import PartitionSpec as P

CF = 2


def pick_live(flat_rows, slot_count, slot_width, row_total):
    running = jnp.cumsum(slot_count).astype(jnp.int32)
    first_slot = running - slot_count
    row_number = jnp.arange(row_total, dtype=jnp.int32)
    source = jnp.sum((running[None, :] <= row_number[:, None]).astype(jnp.int32), axis=1)
    flat_index = source * slot_width + row_number - first_slot[source]
    return flat_rows[flat_index]


def shards(cotangent, slot_token, slot_gate, w_down):
    slot_index = slot_token[0]
    live_slot = slot_index >= 0
    gate_value = jnp.where(live_slot, slot_gate[0], jnp.float32(0.0))
    token_rows = cotangent[jnp.maximum(slot_index, 0)]
    scaled = (gate_value[:, :, None] * token_rows.astype(jnp.float32)).astype(jnp.bfloat16)
    slot_count = jnp.sum(live_slot.astype(jnp.int32), axis=1)
    arrived, arrived_counts = (
        lax.all_to_all(scaled, "expert", split_axis=0, concat_axis=0, tiled=True),
        lax.all_to_all(slot_count, "expert", split_axis=0, concat_axis=0, tiled=True),
    )
    weight = w_down[0]
    slot_width = arrived.shape[1]
    feature_count = arrived.shape[2]
    group_rows = CF * cotangent.shape[0]
    compact = pick_live(arrived.reshape(-1, feature_count), arrived_counts, slot_width, group_rows)
    result = jnp.einsum(
        "rd,fd->rf",
        lax.all_gather(compact, "hidden", axis=0, tiled=True),
        weight,
        preferred_element_type=jnp.float32,
    ).astype(jnp.bfloat16)
    return result[None]


def solution(mesh):
    in_specs = (
        P(("expert", "hidden"), None),
        P(("expert", "hidden"), None, None),
        P(("expert", "hidden"), None, None),
        P("expert", "hidden", None),
    )
    out_specs = P("expert", None, "hidden")
    return jax.shard_map(shards, mesh=mesh, in_specs=in_specs, out_specs=out_specs, check_vma=False)
```

profile of v0, /device:TPU:1, one launch (start us, length us, event | category | flops | bytes accessed | tf_op | source)
XLA Modules:
  0.0 334.0 jit_solution(7072492235129982869)
XLA Ops:
  6.5 0.0 copy-start
  6.5 0.8 fusion.4
  7.3 0.7 copy.20
  8.0 15.6 %all-to-all-start.1 = ((s32[64,1,1]{2,1,0:T(1,128)}), s32[64,1,1]{2,1,0:T(1,128)S(1)}, u32[]{:S(2)}, u32[]{:S(2)}) async-start(s32[64,1,1]{2,1,0:T(1,128)} %copy.20), calls=%async_computation.1 | async-start | bytes 65536 | tf_op jit(solution)/shard_map/all_to_all | solution.py:27
  23.7 0.1 copy.19
  23.7 0.1 reshape.104
  23.9 0.0 copy-done
  23.9 4.1 %gather_fusion = bf16[640,2048]{1,0:T(8,128)(2,1)} fusion(bf16[256,2048]{1,0:T(8,128)(2,1)S(1)} %copy-done, s32[1024]{0:T(1024)S(1)} %pad_clamp_fusion.1), kind=kCustom, calls=%fused_computation | custom fusion | bytes 5245440 | tf_op jit(solution)/shard_map/gather | solution.py:22
  28.0 0.0 copy-start.1
  28.0 0.0 copy-start.2
  28.0 5.8 %reshape.192 = f32[64,10,2048]{2,1,0:T(8,128)} reshape(bf16[640,2048]{1,0:T(8,128)(2,1)} %gather_fusion) | data formatting | bytes 7864320 | tf_op jit(solution)/shard_map/convert_element_type | solution.py:23
  33.8 0.0 copy-done.1
  33.8 0.0 copy-done.2
  33.8 0.1 copy.22
  33.9 5.9 %multiply_convert_fusion = bf16[64,10,2048]{2,1,0:T(8,128)(2,1)} fusion(f32[64,10,2048]{2,1,0:T(8,128)} %reshape.192, f32[64,10]{1,0:T(8,128)S(1)} %bitcast.80), kind=kLoop, calls=%fused_computation.2 | loop fusion | flops 2621440 | bytes 7866880 | tf_op jit(solution)/shard_map/convert_element_type | solution.py:23
  39.8 0.0 all-to-all-done.1
  39.8 13.0 %all-to-all-start = ((bf16[64,10,2048]{2,1,0:T(8,128)(2,1)}), bf16[64,10,2048]{2,1,0:T(8,128)(2,1)}, u32[]{:S(2)}, u32[]{:S(2)}) async-start(bf16[64,10,2048]{2,1,0:T(8,128)(2,1)} %multiply_convert_fusion), calls=%async_computation | async-start | bytes 8388608 | tf_op jit(solution)/shard_map/all_to_all | solution.py:26
  52.9 0.2 all-gather.3.cloned.1.call-start
  53.1 0.1 reduce-window.8
  53.2 0.1 reduce.1
  53.3 1.2 reduce.3
  54.5 0.7 fusion.8
  55.2 0.7 fusion.7
  55.9 0.7 fusion.5
  56.6 0.7 fusion.6
  57.4 0.1 convert_reduce_fusion
  57.5 4.5 %compare_select_fusion.3 = (s32[512,1]{0,1:T(1,128)S(1)}, s32[512,1]{0,1:T(1,128)S(1)}) fusion(s32[]{:T(128)} %bitcast.61, s32[]{:T(128)} %bitcast.62, s32[]{:T(128)} %bitcast.63, s32[]{:T(128)} %bitcast.64, s32[]{:T(128)} %bitcast.65, s32[]{:T(128)} %bitcast.67, s32[]{:T(128)} %bitcast.66, s32[512,1]{0,1:T(1,128)S(1)} %bitcast.81), kind=kLoop, calls=%fused_computation.69 | loop fusion | flops 7680 | bytes 6172 | tf_op jit(solution)/shard_map/gather | solution.py:14
  62.0 0.4 compare_reduce_fusion.56
  62.4 35.5 %select_select_fusion = s32[512]{0:T(512)S(1)} fusion(pred[512]{0:T(512)(128)(4,1)S(1)} %get-tuple-element.61, pred[512]{0:T(512)(128)(4,1)S(1)} %get-tuple-element.60, pred[512]{0:T(512)(128)(4,1)S(1)} %get-tuple-element.59, pred[512]{0:T(512)(128)(4,1)S(1)} %get-tuple-element.58, pred[512]{0:T(512)(128)(4,1)S(1)} %get-tuple-element.57, ...), kind=kLoop, calls=%fused_computation.79 | loop fusion | flops 29184 | bytes 33508 | tf_op jit(solution)/shard_map/gather | solution.py:14
  98.0 50.4 %all-to-all-done = bf16[64,10,2048]{2,1,0:T(8,128)(2,1)} async-done(((bf16[64,10,2048]{2,1,0:T(8,128)(2,1)}), bf16[64,10,2048]{2,1,0:T(8,128)(2,1)}, u32[]{:S(2)}, u32[]{:S(2)}) %all-to-all-start) | async-done | bytes 2621472 | tf_op jit(solution)/shard_map/all_to_all | solution.py:26
  148.4 5.5 %reshape.99 = bf16[640,2048]{1,0:T(8,128)(2,1)} reshape(bf16[64,10,2048]{2,1,0:T(8,128)(2,1)} %all-to-all-done) | data formatting | bytes 5242880 | tf_op jit(solution)/shard_map/reshape | solution.py:33
  153.9 7.3 %gather_fusion.1 = bf16[512,2048]{1,0:T(8,128)(2,1)} fusion(bf16[640,2048]{1,0:T(8,128)(2,1)} %reshape.99, s32[1024]{0:T(1024)S(1)} %pad_clamp_fusion), kind=kCustom, calls=%fused_computation.1 | custom fusion | bytes 4196352 | tf_op jit(solution)/shard_map/gather | solution.py:15
  161.2 0.0 all-gather.3.cloned.1.call-update
  161.2 152.1 %all-gather.3.cloned.1.call-done = bf16[2048,2048]{1,0:T(8,128)(2,1)} async-done(((bf16[512,2048]{1,0:T(8,128)(2,1)}), bf16[2048,2048]{1,0:T(8,128)(2,1)}) %all-gather.3.cloned.1.call-update) | async-done | bytes 8388624 | tf_op jit(solution)/shard_map/all_gather | solution.py:36
  313.3 13.9 %convert_bitcast_fusion = bf16[1,2048,1024]{2,1,0:T(8,128)(2,1)} fusion(bf16[2048,2048]{1,0:T(8,128)(2,1)} %all-gather.3.cloned.1.call-done, bf16[1,1024,2048]{2,1,0:T(8,128)(2,1)} %param.7), kind=kOutput, calls=%fused_computation.5 | convolution fusion | flops 8592031744 | bytes 16777216 | tf_op jit(solution)/shard_map/rd,fd->rf/dot_general | solution.py:34
  (5 shorter events, 0.0 us)
Async XLA Ops:
  6.5 17.4 %copy-start = (bf16[256,2048]{1,0:T(8,128)(2,1)S(1)}, bf16[256,2048]{1,0:T(8,128)(2,1)}, u32[]{:S(2)}) copy-start(bf16[256,2048]{1,0:T(8,128)(2,1)} %param.4) | copy-start | bytes 3145732
  8.0 31.8 %all-to-all-start.1 = ((s32[64,1,1]{2,1,0:T(1,128)}), s32[64,1,1]{2,1,0:T(1,128)S(1)}, u32[]{:S(2)}, u32[]{:S(2)}) async-start(s32[64,1,1]{2,1,0:T(1,128)} %copy.20), calls=%async_computation.1 | async-start | bytes 65536 | tf_op jit(solution)/shard_map/all_to_all | solution.py:27
  28.0 5.9 %copy-start.1 = (s32[1,64,10]{1,0,2:T(1,128)S(1)}, s32[1,64,10]{1,0,2:T(1,128)}, u32[]{:S(2)}) copy-start(s32[1,64,10]{1,0,2:T(1,128)} %param.5) | copy-start | bytes 7684
  28.0 5.9 %copy-start.2 = (f32[1,64,10]{1,0,2:T(1,128)S(1)}, f32[1,64,10]{1,0,2:T(1,128)}, u32[]{:S(2)}) copy-start(f32[1,64,10]{1,0,2:T(1,128)} %param.6) | copy-start | bytes 7684
  39.8 108.5 %all-to-all-start = ((bf16[64,10,2048]{2,1,0:T(8,128)(2,1)}), bf16[64,10,2048]{2,1,0:T(8,128)(2,1)}, u32[]{:S(2)}, u32[]{:S(2)}) async-start(bf16[64,10,2048]{2,1,0:T(8,128)(2,1)} %multiply_convert_fusion), calls=%async_computation | async-start | bytes 8388608 | tf_op jit(solution)/shard_map/all_to_all | solution.py:26
  52.9 260.5 %all-gather.3.cloned.1.call-start = ((), (), s32[]{:S(2)}) async-start(), calls=%async_computation.2 | async-start | bytes 10485760 | tf_op jit(solution)/shard_map/all_gather | solution.py:36
Sparse Core Ops, SparseCore 0:
  161.3 151.9 all-gather.2
where the time goes:
time: 335 us; the launch traced here: 334 us
  waiting for transfers between devices  203 us (61%)
  other arithmetic  48.7 us (15%)
  starting transfers between devices  28.8 us (9%)
  local copies, waits for them, and re-layouts  26.6 us (8%)
  matrix products  13.9 us (4%)
  between operations  13.5 us (4%)
    all_gather x1, waiting for transfers between devices, shards(): lax.all_gather(compact, 'hidden', axis=0, tiled=True)  152 us
    all_to_all x1, waiting for transfers between devices, shards(): lax.all_to_all(scaled, 'expert', split_axis=0, concat_axis=0, tiled=True)  50.4 us
    gather x3, other arithmetic, pick_live(): flat_index = source * slot_width + row_number - first_slot[source]  40.4 us
    all_to_all x1, starting transfers between devices, shards(): lax.all_to_all(slot_count, 'expert', split_axis=0, concat_axis=0, tiled=T...  15.6 us
    dot_general x1, matrix products, shards(): jnp.einsum('rd,fd->rf', lax.all_gather(compact, 'hidden', axis=0, tiled=T...  13.9 us
    all_to_all x1, starting transfers between devices, shards(): lax.all_to_all(scaled, 'expert', split_axis=0, concat_axis=0, tiled=True)  13 us
    gather x1, local copies, waits for them, and re-layouts, pick_live(): return flat_rows[flat_index]  7.31 us
  transfers between devices with their start and end apart: 3, of which 2 were waited for; matrix products, arithmetic and copies ran while one was open for 18% of the time, Pallas kernels for 0%

commit v1 on v0

v1 whole, which is shorter than its diff:
```python
import jax
import jax.numpy as jnp
from jax import lax
from jax.sharding import Mesh, PartitionSpec as P

AXES = ("zhi", "y", "x", "core", "zlo")
COLUMN = ("zhi", "zlo")
PLANE = ("y", "x", "core")
CHUNKS = (512, 512, 512, 512)
DEAD = 128.0


def shards(cotangent, slot_token, slot_gate, w_down):
    tokens, features = cotangent.shape
    experts, width = slot_token.shape[1:]
    planes = 8
    half = experts // 2
    rows = half * planes * width
    hidden = w_down.shape[1]

    table = jnp.concatenate([slot_token.astype(jnp.float32).reshape(1, -1), slot_gate.reshape(1, -1)], axis=1)
    table = lax.all_gather(table, COLUMN, axis=0, tiled=True).reshape(planes, 2, experts, width)
    table = lax.dynamic_slice_in_dim(table, lax.axis_index("zhi") * half, half, axis=2)
    slot = jnp.transpose(table[:, 0], (1, 0, 2)).astype(jnp.int32)
    gate = jnp.transpose(table[:, 1], (1, 0, 2)).reshape(rows, 1)
    live = (slot >= 0).reshape(rows, 1)
    row = (slot + tokens * jnp.arange(planes, dtype=jnp.int32)[None, :, None]).reshape(rows, 1)
    row = jnp.where(live, row, -1)
    pick = (row == jnp.arange(planes * tokens, dtype=jnp.int32)[None, :]).astype(jnp.bfloat16)

    total = None
    place = None
    start = 0
    for chunk in CHUNKS:
        part = lax.all_gather(cotangent[:, start : start + chunk], COLUMN, axis=0, tiled=True)
        picked = jnp.dot(pick, part, preferred_element_type=jnp.float32)
        scaled = jnp.where(live, gate * picked, DEAD).astype(jnp.bfloat16)
        arrived = lax.all_to_all(scaled, PLANE, split_axis=0, concat_axis=0, tiled=True)
        if place is None:
            alive = (arrived[:, 0] < 64.0).astype(jnp.int32).reshape(half, 2, 4, width)
            alive = jnp.transpose(alive, (2, 1, 0, 3)).reshape(-1)
            at = jnp.where(alive > 0, jnp.cumsum(alive) - 1, -1)
            at = jnp.transpose(at.reshape(4, 2, half, width), (2, 1, 0, 3)).reshape(1, rows)
            place = (at == jnp.arange(planes * tokens, dtype=jnp.int32)[:, None]).astype(jnp.bfloat16)
        term = lax.dot_general(
            arrived, w_down[0, :, start : start + chunk], (((1,), (1,)), ((), ())), preferred_element_type=jnp.float32
        )
        total = term if total is None else total + term
        start += chunk
    result = jnp.dot(place, total.astype(jnp.bfloat16), preferred_element_type=jnp.float32)
    return result.astype(jnp.bfloat16)[None]


def solution(mesh):
    fine = Mesh(mesh.devices.reshape(2, 4, 4, 2, 4), AXES)
    wide = ("zhi", "y", "x", "core")
    in_specs = (P(AXES, None), P(AXES, None, None), P(AXES, None, None), P(wide, "zlo", None))
    return jax.shard_map(shards, mesh=fine, in_specs=in_specs, out_specs=P(wide, None, "zlo"), check_vma=False)
```

time: 335 us -> 264 us (0.79)
  waiting for transfers between devices: 203 us -> 95 us
  matrix products: 13.9 us -> 88.1 us
  other arithmetic: 48.7 us -> 2.94 us
  blocking collectives: 0 us -> 24.4 us
  local copies, waits for them, and re-layouts: 26.6 us -> 6.79 us
  starting transfers between devices: 28.8 us -> 32.8 us
    all_gather x1 -> x4, waiting for transfers between devices: 152 us -> 67.8 us  [shards(): lax.all_gather(cotangent[:, start:start + chunk], COLUMN, axis=0, tiled=T...]
    dot_general x1 -> x9, matrix products: 13.9 us -> 88.1 us  [the longest x4 38.3 us: shards(): picked = jnp.dot(pick, part, preferred_element_type=jnp.float32)]
    gather x5 -> x0, other arithmetic: 40.4 us -> none  [the longest x3 40.4 us: pick_live(): flat_index = source * slot_width + row_number - first_slot[source]]
    all_to_all x2 -> x4, waiting for transfers between devices: 50.4 us -> 25.2 us  [shards(): lax.all_to_all(scaled, PLANE, split_axis=0, concat_axis=0, tiled=True)]
    all_gather x0 -> x1, blocking collectives: none -> 24.4 us  [shards(): lax.all_gather(table, COLUMN, axis=0, tiled=True)]
    gather x6 -> x0, local copies, waits for them, and re-layouts: 14.2 us -> none  [the longest x1 7.31 us: pick_live(): return flat_rows[flat_index]]
    convert_element_type x1, local copies, waits for them, and re-layouts: 5.85 us -> 0.1 us  [shards(): slot_token.astype(jnp.float32).reshape(1, -1)]
    convert_element_type x1, other arithmetic: 5.91 us -> 0.7 us  [shards(): slot_token.astype(jnp.float32).reshape(1, -1)]
  transfers between devices with their start and end apart: 3 -> 8, of which waited for: 2 -> 8; matrix products, arithmetic and copies ran while one was open for 18% -> 25% of each run, Pallas kernels for 0% -> 0%
where the time goes in v1:
time: 264 us; the launch traced here: 263 us
  waiting for transfers between devices  95 us (36%)
  matrix products  88.1 us (33%)
  starting transfers between devices  32.8 us (12%)
  blocking collectives  24.4 us (9%)
  between operations  13.3 us (5%)
  local copies, waits for them, and re-layouts  6.79 us (3%)
  other arithmetic  2.94 us (1%)
    all_gather x4, waiting for transfers between devices, shards(): lax.all_gather(cotangent[:, start:start + chunk], COLUMN, axis=0, tiled=T...  67.8 us
    dot_general x4, matrix products, shards(): picked = jnp.dot(pick, part, preferred_element_type=jnp.float32)  38.3 us
    dot_general x4, matrix products, shards(): lax.dot_general(arrived, w_down[0, :, start:start + chunk], (((1,), (1,))...  35.6 us
    all_to_all x4, starting transfers between devices, shards(): lax.all_to_all(scaled, PLANE, split_axis=0, concat_axis=0, tiled=True)  32.7 us
    all_to_all x4, waiting for transfers between devices, shards(): lax.all_to_all(scaled, PLANE, split_axis=0, concat_axis=0, tiled=True)  25.2 us
    all_gather x1, blocking collectives, shards(): lax.all_gather(table, COLUMN, axis=0, tiled=True)  24.4 us
    dot_general x1, matrix products, shards(): jnp.dot(place, total.astype(jnp.bfloat16), preferred_element_type=jnp.flo...  14.3 us
  transfers between devices with their start and end apart: 8, of which 8 were waited for; matrix products, arithmetic and copies ran while one was open for 25% of the time, Pallas kernels for 0%

profile of v1, /device:TPU:1, one launch (start us, length us, event | category | flops | bytes accessed | tf_op | source)
XLA Modules:
  0.0 263.4 jit_solution(712971367003464215)
XLA Ops:
  6.5 0.0 all-gather.10.cloned.1.call-start
  6.5 2.2 fusion.23
  8.7 0.0 all-gather.10.cloned.1.call-update
  8.7 0.0 all-gather.6.cloned.1.call-start
  8.8 0.7 all-gather.6.cloned.1.call-update
  9.5 0.0 all-gather.8.cloned.1.call-start
  9.5 0.7 all-gather.8.cloned.1.call-update
  10.2 0.7 convert_element_type.35
  10.9 0.1 copy.20
  11.0 0.1 reshape.71
  11.2 0.8 copy.21
  11.9 0.1 reshape.72
  12.1 24.4 %all-gather = f32[8,1,1280]{2,1,0:T(1,128)S(1)} all-gather(f32[1,1,1280]{2,1,0:T(1,128)S(1)} %maximum_bitcast_fusion), channel_id=1, replica_groups=mesh['zhi'=2,'y'=4,'x'=4,'core'=2,'zlo'=4] {'zhi','zlo'}, dimensions={0}, use_global_device_ids=true | all-gather | bytes 46080 | tf_op jit(solution)/shard_map/all_gather | solution.py:22
  36.5 0.1 reduce
  36.6 0.5 reshape.73
  37.2 0.2 broadcast_in_dim.38
  37.3 0.1 copy.23
  37.4 0.1 mul.40
  37.6 0.1 add_bitcast_fusion
  37.7 0.1 copy.24
  37.7 0.1 reshape.74
  37.9 11.4 %all-gather.10.cloned.1.call-done = bf16[2048,512]{1,0:T(8,128)(2,1)} async-done(((bf16[256,512]{1,0:T(8,128)(2,1)}), bf16[2048,512]{1,0:T(8,128)(2,1)}) %all-gather.10.cloned.1.call-update) | async-done | bytes 2097168 | tf_op jit(solution)/shard_map/all_gather | solution.py:35
  49.3 9.6 %select_convert_fusion.1 = bf16[2560,512]{1,0:T(8,128)(2,1)} fusion(bf16[2048,512]{1,0:T(8,128)(2,1)} %all-gather.10.cloned.1.call-done, s32[2560]{0:T(1024)S(1)} %broadcast_select_fusion, f32[2560]{0:T(1024)S(1)} %mul.40, pred[2560]{0:T(1024)(128)(4,1)S(1)} %broadcast_in_dim.38), kind=kOutput, calls=%fused_computation.14 | convolution fusion | flops 5377884160 | bytes 4741632 | tf_op jit(solution)/shard_map/dot_general | solution.py:36
  58.8 12.1 %all-to-all-start.2 = ((bf16[32,80,512]{2,1,0:T(8,128)(2,1)}), bf16[32,80,512]{2,1,0:T(8,128)(2,1)S(1)}, u32[]{:S(2)}, u32[]{:S(2)}) async-start(bf16[32,80,512]{2,1,0:T(8,128)(2,1)} %bitcast.58), calls=%async_computation.2 | async-start | bytes 5242880 | tf_op jit(solution)/shard_map/all_to_all | solution.py:38
  70.9 0.0 all-gather.12.cloned.1.call-start
  71.0 0.5 all-gather.12.cloned.1.call-update
  71.5 19.5 %all-gather.6.cloned.1.call-done = bf16[2048,512]{1,0:T(8,128)(2,1)} async-done(((bf16[256,512]{1,0:T(8,128)(2,1)}), bf16[2048,512]{1,0:T(8,128)(2,1)}) %all-gather.6.cloned.1.call-update) | async-done | bytes 2097168 | tf_op jit(solution)/shard_map/all_gather | solution.py:35
  91.0 9.6 %select_convert_fusion.3 = bf16[2560,512]{1,0:T(8,128)(2,1)} fusion(bf16[2048,512]{1,0:T(8,128)(2,1)} %all-gather.6.cloned.1.call-done, s32[2560]{0:T(1024)S(1)} %broadcast_select_fusion, f32[2560]{0:T(1024)S(1)} %mul.40, pred[2560]{0:T(1024)(128)(4,1)S(1)} %broadcast_in_dim.38), kind=kOutput, calls=%fused_computation.16 | convolution fusion | flops 5377884160 | bytes 4741632 | tf_op jit(solution)/shard_map/dot_general | solution.py:36
  100.5 4.3 %all-to-all-done.2 = bf16[32,80,512]{2,1,0:T(8,128)(2,1)S(1)} async-done(((bf16[32,80,512]{2,1,0:T(8,128)(2,1)}), bf16[32,80,512]{2,1,0:T(8,128)(2,1)S(1)}, u32[]{:S(2)}, u32[]{:S(2)}) %all-to-all-start.2) | async-done | bytes 2621472 | tf_op jit(solution)/shard_map/all_to_all | solution.py:38
  104.9 0.0 copy-start.1
  104.9 1.5 copy-done.1
  106.4 7.5 %all-to-all-start = ((bf16[32,80,512]{2,1,0:T(8,128)(2,1)}), bf16[32,80,512]{2,1,0:T(8,128)(2,1)S(1)}, u32[]{:S(2)}, u32[]{:S(2)}) async-start(bf16[32,80,512]{2,1,0:T(8,128)(2,1)} %bitcast.60), calls=%async_computation | async-start | bytes 5242880 | tf_op jit(solution)/shard_map/all_to_all | solution.py:38
  113.9 18.3 %all-gather.8.cloned.1.call-done = bf16[2048,512]{1,0:T(8,128)(2,1)} async-done(((bf16[256,512]{1,0:T(8,128)(2,1)}), bf16[2048,512]{1,0:T(8,128)(2,1)}) %all-gather.8.cloned.1.call-update) | async-done | bytes 2097168 | tf_op jit(solution)/shard_map/all_gather | solution.py:35
  132.2 9.6 %select_convert_fusion.2 = bf16[2560,512]{1,0:T(8,128)(2,1)} fusion(bf16[2048,512]{1,0:T(8,128)(2,1)} %all-gather.8.cloned.1.call-done, s32[2560]{0:T(1024)S(1)} %broadcast_select_fusion, f32[2560]{0:T(1024)S(1)} %mul.40, pred[2560]{0:T(1024)(128)(4,1)S(1)} %broadcast_in_dim.38), kind=kOutput, calls=%fused_computation.15 | convolution fusion | flops 5377884160 | bytes 4741632 | tf_op jit(solution)/shard_map/dot_general | solution.py:36
  141.8 6.0 %all-to-all-done = bf16[32,80,512]{2,1,0:T(8,128)(2,1)S(1)} async-done(((bf16[32,80,512]{2,1,0:T(8,128)(2,1)}), bf16[32,80,512]{2,1,0:T(8,128)(2,1)S(1)}, u32[]{:S(2)}, u32[]{:S(2)}) %all-to-all-start) | async-done | bytes 2621472 | tf_op jit(solution)/shard_map/all_to_all | solution.py:38
  147.8 0.0 copy-start
  147.8 6.9 %all-to-all-start.1 = ((bf16[32,80,512]{2,1,0:T(8,128)(2,1)}), bf16[32,80,512]{2,1,0:T(8,128)(2,1)}, u32[]{:S(2)}, u32[]{:S(2)}) async-start(bf16[32,80,512]{2,1,0:T(8,128)(2,1)} %bitcast.59), calls=%async_computation.1 | async-start | bytes 5242880 | tf_op jit(solution)/shard_map/all_to_all | solution.py:38
  154.7 18.6 %all-gather.12.cloned.1.call-done = bf16[2048,512]{1,0:T(8,128)(2,1)} async-done(((bf16[256,512]{1,0:T(8,128)(2,1)}), bf16[2048,512]{1,0:T(8,128)(2,1)}) %all-gather.12.cloned.1.call-update) | async-done | bytes 2097168 | tf_op jit(solution)/shard_map/all_gather | solution.py:35
  173.3 9.6 %select_convert_fusion = bf16[2560,512]{1,0:T(8,128)(2,1)} fusion(bf16[2048,512]{1,0:T(8,128)(2,1)} %all-gather.12.cloned.1.call-done, s32[2560]{0:T(1024)S(1)} %broadcast_select_fusion, f32[2560]{0:T(1024)S(1)} %mul.40, pred[2560]{0:T(1024)(128)(4,1)S(1)} %broadcast_in_dim.38), kind=kOutput, calls=%fused_computation.13 | convolution fusion | flops 5377884160 | bytes 4741632 | tf_op jit(solution)/shard_map/dot_general | solution.py:36
  182.9 0.0 copy-done
  182.9 5.8 %all-to-all-done.1 = bf16[32,80,512]{2,1,0:T(8,128)(2,1)} async-done(((bf16[32,80,512]{2,1,0:T(8,128)(2,1)}), bf16[32,80,512]{2,1,0:T(8,128)(2,1)}, u32[]{:S(2)}, u32[]{:S(2)}) %all-to-all-start.1) | async-done | bytes 2621472 | tf_op jit(solution)/shard_map/all_to_all | solution.py:38
  188.7 6.3 %all-to-all-start.3 = ((bf16[32,80,512]{2,1,0:T(8,128)(2,1)}), bf16[32,80,512]{2,1,0:T(8,128)(2,1)S(1)}, u32[]{:S(2)}, u32[]{:S(2)}) async-start(bf16[32,80,512]{2,1,0:T(8,128)(2,1)} %bitcast.57), calls=%async_computation.3 | async-start | bytes 5242880 | tf_op jit(solution)/shard_map/all_to_all | solution.py:38
  195.0 1.5 convert_reduce_fusion
  196.5 0.2 reshape.77
  196.8 0.1 reshape.75
  196.9 0.3 reduce-window.9
  197.2 0.1 slice.54
  197.3 0.1 slice_reduce_fusion
  197.4 0.1 add_add_fusion
  197.5 0.2 sub.7
  197.6 0.1 fusion.22
  197.8 0.2 eq.31
  197.9 0.0 copy-start.3
  197.9 9.1 %fusion.15 = f32[2560,1024]{1,0:T(8,128)} fusion(bf16[2560,512]{1,0:T(8,128)(2,1)} %bitcast.55, bf16[1,1024,2048]{2,1,0:T(8,128)(2,1)} %param.7), kind=kOutput, calls=%fused_computation.24 | convolution fusion | flops 2684354560 | bytes 14155776 | tf_op jit(solution)/shard_map/dot_general | solution.py:45
  207.0 0.0 copy-done.3
  207.0 0.0 copy-start.2
  207.0 7.4 %fusion.13 = f32[2560,1024]{1,0:T(8,128)} fusion(bf16[2560,512]{1,0:T(8,128)(2,1)} %bitcast.12, bf16[1,1024,2048]{2,1,0:T(8,128)(2,1)S(1)} %copy-done.3), kind=kOutput, calls=%fused_computation.22 | convolution fusion | flops 2684354560 | bytes 14155776 | tf_op jit(solution)/shard_map/dot_general | solution.py:45
  214.4 0.0 copy-done.2
  214.5 5.5 %fusion.11 = f32[2560,1024]{1,0:T(8,128)} fusion(bf16[2560,512]{1,0:T(8,128)(2,1)S(1)} %bitcast.56, bf16[1,1024,2048]{2,1,0:T(8,128)(2,1)S(1)} %copy-done.3), kind=kOutput, calls=%fused_computation.20 | convolution fusion | flops 2684354560 | bytes 14155776 | tf_op jit(solution)/shard_map/dot_general | solution.py:45
  220.0 9.0 %all-to-all-done.3 = bf16[32,80,512]{2,1,0:T(8,128)(2,1)S(1)} async-done(((bf16[32,80,512]{2,1,0:T(8,128)(2,1)}), bf16[32,80,512]{2,1,0:T(8,128)(2,1)S(1)}, u32[]{:S(2)}, u32[]{:S(2)}) %all-to-all-start.3) | async-done | bytes 2621472 | tf_op jit(solution)/shard_map/all_to_all | solution.py:38
  229.0 13.6 %add_convert_fusion = bf16[2560,1024]{1,0:T(8,128)(2,1)} fusion(f32[2560,1024]{1,0:T(8,128)} %fusion.11, f32[2560,1024]{1,0:T(8,128)} %fusion.15, f32[2560,1024]{1,0:T(8,128)} %fusion.13, bf16[2560,512]{1,0:T(8,128)(2,1)S(1)} %bitcast.53, bf16[1,1024,2048]{2,1,0:T(8,128)(2,1)} %param.7), kind=kOutput, calls=%fused_computation.7 | convolution fusion | flops 2694840320 | bytes 40370176 | tf_op jit(solution)/shard_map/dot_general | solution.py:45
  242.6 14.3 %convert_bitcast_fusion = bf16[1,2048,1024]{2,1,0:T(8,128)(2,1)} fusion(bf16[2560,1024]{1,0:T(8,128)(2,1)} %add_convert_fusion, s32[2560]{0:T(1024)S(1)} %eq.31), kind=kOutput, calls=%fused_computation.17 | convolution fusion | flops 10744758272 | bytes 9447424 | tf_op jit(solution)/shard_map/dot_general | solution.py:50
  (8 shorter events, 0.2 us)
Async XLA Ops:
  6.5 42.7 %all-gather.10.cloned.1.call-start = ((), (), s32[]{:S(2)}) async-start(), calls=%async_computation.6 | async-start | bytes 2359296 | tf_op jit(solution)/shard_map/all_gather | solution.py:35
  8.7 82.2 %all-gather.6.cloned.1.call-start = ((), (), s32[]{:S(2)}) async-start(), calls=%async_computation.4 | async-start | bytes 2359296 | tf_op jit(solution)/shard_map/all_gather | solution.py:35
  9.5 122.7 %all-gather.8.cloned.1.call-start = ((), (), s32[]{:S(2)}) async-start(), calls=%async_computation.5 | async-start | bytes 2359296 | tf_op jit(solution)/shard_map/all_gather | solution.py:35
  58.8 46.1 %all-to-all-start.2 = ((bf16[32,80,512]{2,1,0:T(8,128)(2,1)}), bf16[32,80,512]{2,1,0:T(8,128)(2,1)S(1)}, u32[]{:S(2)}, u32[]{:S(2)}) async-start(bf16[32,80,512]{2,1,0:T(8,128)(2,1)} %bitcast.58), calls=%async_computation.2 | async-start | bytes 5242880 | tf_op jit(solution)/shard_map/all_to_all | solution.py:38
  70.9 102.4 %all-gather.12.cloned.1.call-start = ((), (), s32[]{:S(2)}) async-start(), calls=%async_computation.7 | async-start | bytes 2359296 | tf_op jit(solution)/shard_map/all_gather | solution.py:35
  104.9 1.5 copy-start.1
  106.4 41.5 %all-to-all-start = ((bf16[32,80,512]{2,1,0:T(8,128)(2,1)}), bf16[32,80,512]{2,1,0:T(8,128)(2,1)S(1)}, u32[]{:S(2)}, u32[]{:S(2)}) async-start(bf16[32,80,512]{2,1,0:T(8,128)(2,1)} %bitcast.60), calls=%async_computation | async-start | bytes 5242880 | tf_op jit(solution)/shard_map/all_to_all | solution.py:38
  147.8 35.1 %copy-start = (bf16[32,80,512]{2,1,0:T(8,128)(2,1)}, bf16[32,80,512]{2,1,0:T(8,128)(2,1)S(1)}, u32[]{:S(2)}) copy-start(bf16[32,80,512]{2,1,0:T(8,128)(2,1)S(1)} %all-to-all-done) | copy-start | bytes 7864324
  147.8 40.9 %all-to-all-start.1 = ((bf16[32,80,512]{2,1,0:T(8,128)(2,1)}), bf16[32,80,512]{2,1,0:T(8,128)(2,1)}, u32[]{:S(2)}, u32[]{:S(2)}) async-start(bf16[32,80,512]{2,1,0:T(8,128)(2,1)} %bitcast.59), calls=%async_computation.1 | async-start | bytes 5242880 | tf_op jit(solution)/shard_map/all_to_all | solution.py:38
  188.7 40.3 %all-to-all-start.3 = ((bf16[32,80,512]{2,1,0:T(8,128)(2,1)}), bf16[32,80,512]{2,1,0:T(8,128)(2,1)S(1)}, u32[]{:S(2)}, u32[]{:S(2)}) async-start(bf16[32,80,512]{2,1,0:T(8,128)(2,1)} %bitcast.57), calls=%async_computation.3 | async-start | bytes 5242880 | tf_op jit(solution)/shard_map/all_to_all | solution.py:38
  197.9 9.1 %copy-start.3 = (bf16[1,1024,2048]{2,1,0:T(8,128)(2,1)S(1)}, bf16[1,1024,2048]{2,1,0:T(8,128)(2,1)}, u32[]{:S(2)}) copy-start(bf16[1,1024,2048]{2,1,0:T(8,128)(2,1)} %param.7) | copy-start | bytes 12582916
  207.0 7.4 %copy-start.2 = (bf16[32,80,512]{2,1,0:T(8,128)(2,1)S(1)}, bf16[32,80,512]{2,1,0:T(8,128)(2,1)}, u32[]{:S(2)}) copy-start(bf16[32,80,512]{2,1,0:T(8,128)(2,1)} %copy-done.1) | copy-start | bytes 7864324
Sparse Core Ops, SparseCore 0:
  9.1 40.0 all-gather.9
  51.0 39.8 all-gather.5
  92.8 39.4 all-gather.7
  133.9 39.4 all-gather.11

commit v2 on v1

v2 whole, which is shorter than its diff:
```python
import functools

import jax
import jax.numpy as jnp
from jax import lax
from jax.experimental import pallas as pl
from jax.experimental.pallas import tpu as pltpu
from jax.sharding import Mesh, PartitionSpec as P


AXES = ("zhi", "y", "x", "core", "zlo")
COLUMN = ("zhi", "zlo")
PLANE = ("y", "x", "core")
PLANES = 8
DEAD = 128.0
HEAD = 8
UP = [(i, (i + 1) % PLANES) for i in range(PLANES)]
DOWN = [(i, (i - 1) % PLANES) for i in range(PLANES)]
GROUPS = (((0,), 4), ((-1, 1), 2), ((-2, 2), 2), ((-3, 3, 4), 1))
TILES = 4
SKIP = 8192
CONTRACT_LAST = (((1,), (1,)), ((), ()))


def ring(a, b):
    return lax.ppermute(a, COLUMN, UP), lax.ppermute(b, COLUMN, DOWN)


def pack_table(slot_token, slot_gate, columns):
    gate = slot_gate.reshape(1, -1)
    high = lax.reduce_precision(gate, 8, 7)
    middle = lax.reduce_precision(gate - high, 8, 7)
    low = gate - high - middle
    table = jnp.concatenate([slot_token.astype(jnp.float32).reshape(1, -1), high, middle, low], axis=0)
    return jnp.pad(table, ((0, HEAD - 4), (0, columns - table.shape[1]))).astype(jnp.bfloat16)


def dispatch_kernel(sources, pieces, half, width, padded, zhi_ref, *refs):
    out_ref = refs[-1]
    parts = refs[:-1]
    columns = out_ref.shape[1]
    each = half // TILES
    rows = each * padded
    slots = 2 * half * width
    whole = sources if len(parts) == sources else sources - 1
    tables = [parts[j][parts[j].shape[0] - HEAD :, :slots] for j in range(sources)]
    first = zhi_ref[0] * half + pl.program_id(0) * each

    def block_of(rem):
        block = jnp.zeros_like(rem)
        for i in range(1, sources * pieces):
            block = block + (rem >= i * width).astype(jnp.int32)
        return block

    shape = (each, padded, slots)
    rem = lax.broadcasted_iota(jnp.int32, shape, 1)
    block = block_of(rem)
    target = (first + lax.broadcasted_iota(jnp.int32, shape, 0)) * width + rem - block * width
    hit = lax.broadcasted_iota(jnp.int32, shape, 2) == target
    data = jnp.zeros((rows, HEAD), jnp.float32)
    for j in range(sources):
        mine = hit & (block >= j * pieces) & (block < (j + 1) * pieces)
        mine = jnp.where(mine, 1.0, 0.0).reshape(rows, slots).astype(jnp.bfloat16)
        data = data + lax.dot_general(mine, tables[j], CONTRACT_LAST, preferred_element_type=jnp.float32)
    token = data[:, 0:1]
    gate = data[:, 1:2] + data[:, 2:3] + data[:, 3:4]
    rem = lax.broadcasted_iota(jnp.int32, (each, padded, 1), 1).reshape(rows, 1)
    block = block_of(rem)
    token = jnp.where(rem < sources * pieces * width, token, -1.0)
    total = None
    for j in range(sources):
        for q in range(pieces):
            token_of = jnp.where(block == j * pieces + q, token, -1.0)
            if j < whole:
                spans = [(parts[j], 0, parts[j].shape[0] - HEAD)]
            else:
                low = parts[-1].shape[0]
                spans = [(parts[-1], 0, low), (parts[j], low, parts[j].shape[0] - HEAD)]
            for ref, base, length in spans:
                lane = lax.broadcasted_iota(jnp.int32, (rows, length), 1).astype(jnp.float32) + float(base)
                pick = jnp.where(lane == token_of, 1.0, 0.0).astype(jnp.bfloat16)
                term = jnp.dot(
                    pick, ref[:length, q * columns : (q + 1) * columns], preferred_element_type=jnp.float32
                )
                total = term if total is None else total + term
    out_ref[...] = jnp.where(token >= 0.0, gate * total, DEAD).astype(jnp.bfloat16)


def dispatch(number, zhi, parts, half, width):
    sources, pieces = GROUPS[number]
    columns = parts[0].shape[1] // pieces
    used = len(sources) * pieces * width
    padded = -(-used // 8) * 8
    rows = half * padded
    depth = sum(p.shape[0] for p in parts)
    return pl.pallas_call(
        functools.partial(dispatch_kernel, len(sources), pieces, half, width, padded),
        grid_spec=pltpu.PrefetchScalarGridSpec(
            num_scalar_prefetch=1,
            grid=(TILES,),
            in_specs=[pl.BlockSpec(p.shape, lambda t, s: (0, 0)) for p in parts],
            out_specs=pl.BlockSpec((rows // TILES, columns), lambda t, s: (t, 0)),
        ),
        out_shape=jax.ShapeDtypeStruct((rows, columns), jnp.bfloat16),
        cost_estimate=pl.CostEstimate(
            flops=2 * rows * depth * columns, bytes_accessed=2 * (depth * pieces + rows) * columns, transcendentals=0
        ),
    )(zhi.reshape(1), *parts)


def places(x_ref, sources, pieces, half, width, share, z):
    rows = x_ref.shape[0]
    padded = rows // half
    first = jnp.where(lax.broadcasted_iota(jnp.int32, (8, 128), 1) == 0, 1.0, 0.0).astype(jnp.bfloat16)
    value = lax.dot_general(first, x_ref[:, :128], CONTRACT_LAST, preferred_element_type=jnp.float32)

    def block_of(shape, axis):
        index = lax.broadcasted_iota(jnp.int32, shape, axis).astype(jnp.float32)
        place = jnp.floor((index + 0.5) * (1.0 / padded))
        return index, jnp.floor((index - place * padded + 0.5) * (1.0 / width))

    index, block = block_of((1, rows), 1)
    index_down, block_down = block_of((rows, 1), 0)
    alive = jnp.where((value < 64.0) & (block < len(sources) * pieces), 1.0, 0.0)
    earlier = jnp.where((block_down == block) & (index_down < index), 1.0, 0.0).astype(jnp.bfloat16)
    code = jnp.dot(alive.astype(jnp.bfloat16), earlier, preferred_element_type=jnp.float32)
    for j, offset in enumerate(sources):
        source = lax.rem(z + (offset + PLANES), PLANES)
        held = jnp.sum(jnp.where(block == j * pieces, alive[0:1], 0.0), axis=1, keepdims=True)
        upper = jnp.where(source >= 4, 1.0, 0.0)
        base = (lax.rem(source, 4) * share).astype(jnp.float32) + upper * (share - held)
        for q in range(pieces):
            code = code + jnp.where(block == j * pieces + q, base + float(SKIP * q), 0.0)
    return jnp.where(alive > 0.0, code, -1.0).astype(jnp.int32)


def chosen(code, share, h, q):
    position = lax.broadcasted_iota(jnp.int32, (share, code.shape[1]), 0) + (h * share + SKIP * q)
    return jnp.where(code == position, 1.0, 0.0).astype(jnp.bfloat16)


def early_kernel(half, width, s_ref, x0_ref, x1_ref, x2_ref, w_ref, out_ref, row_ref, c0_ref, c1_ref):
    i = pl.program_id(0)
    share = out_ref.shape[0]
    h = s_ref[1 + i]

    def route(number, x_ref, c_ref, fresh):
        sources, pieces = GROUPS[number]

        @pl.when(fresh)
        def _():
            c_ref[...] = places(x_ref, sources, pieces, half, width, share, s_ref[0])

        columns = x_ref.shape[1]
        for q in range(pieces):
            row_ref[:, q * columns : (q + 1) * columns] = jnp.dot(
                chosen(c_ref[0:1, :], share, h, q), x_ref[...], preferred_element_type=jnp.float32
            ).astype(jnp.bfloat16)

    @pl.when(i == 0)
    def _():
        route(0, x0_ref, c0_ref, i == 0)

    @pl.when((i == 1) | (i == 2))
    def _():
        route(1, x1_ref, c1_ref, i == 1)

    @pl.when(i == 3)
    def _():
        route(2, x2_ref, c0_ref, i == 3)

    out_ref[...] = lax.dot_general(
        row_ref[...], w_ref[...], CONTRACT_LAST, preferred_element_type=jnp.float32
    ).astype(jnp.bfloat16)


def early(z, x0, x1, x2, weight, half, width, share):
    hidden, features = weight.shape
    rows = x1.shape[0]
    order = jnp.stack([z, z % 4, (z - 1) % 4, (z + 1) % 4, (z + 2) % 4])
    return pl.pallas_call(
        functools.partial(early_kernel, half, width),
        grid_spec=pltpu.PrefetchScalarGridSpec(
            num_scalar_prefetch=1,
            grid=(4,),
            in_specs=[pl.BlockSpec(a.shape, lambda i, s: (0, 0)) for a in (x0, x1, x2, weight)],
            out_specs=pl.BlockSpec((share, hidden), lambda i, s: (s[1 + i], 0)),
            scratch_shapes=[
                pltpu.VMEM((share, features), jnp.bfloat16),
                pltpu.VMEM((8, rows), jnp.int32),
                pltpu.VMEM((8, rows), jnp.int32),
            ],
        ),
        out_shape=jax.ShapeDtypeStruct((4 * share, hidden), jnp.bfloat16),
        name="early",
        cost_estimate=pl.CostEstimate(
            flops=8 * share * features * (rows + hidden), bytes_accessed=4 * features * (rows + hidden), transcendentals=0
        ),
        compiler_params=pltpu.CompilerParams(vmem_limit_bytes=56 << 20),
    )(order, x0, x1, x2, weight)


def late_kernel(half, width, steps, s_ref, front_ref, x_ref, w_ref, old_ref, out_ref, c_ref, y_ref):
    i = pl.program_id(0)
    share = out_ref.shape[0]
    tile = x_ref.shape[0]

    @pl.when(i == 0)
    def _():
        c_ref[...] = places(front_ref, GROUPS[3][0], 1, half, width, share, s_ref[0])

    @pl.when(i < steps)
    def _():
        y_ref[pl.ds(pl.multiple_of(i * tile, 16), tile), :] = lax.dot_general(
            x_ref[...], w_ref[...], CONTRACT_LAST, preferred_element_type=jnp.float32
        ).astype(jnp.bfloat16)

    @pl.when(i >= steps)
    def _():
        h = s_ref[1 + jnp.maximum(i - steps, 0)]
        out = jnp.dot(chosen(c_ref[0:1, :], share, h, 0), y_ref[...], preferred_element_type=jnp.float32)
        out_ref[...] = (out + old_ref[...].astype(jnp.float32)).astype(jnp.bfloat16)


def late(z, x, weight, old, half, width, share):
    hidden, features = weight.shape
    rows = x.shape[0]
    steps = 4
    order = jnp.stack([z] + [(z + offset) % 4 for offset in GROUPS[3][0]])
    count = len(GROUPS[3][0])
    tile = pl.BlockSpec((share, hidden), lambda i, s: (s[1 + jnp.maximum(i - steps, 0)], 0))
    return pl.pallas_call(
        functools.partial(late_kernel, half, width, steps),
        grid_spec=pltpu.PrefetchScalarGridSpec(
            num_scalar_prefetch=1,
            grid=(steps + count,),
            in_specs=[
                pl.BlockSpec((rows, 128), lambda i, s: (0, 0)),
                pl.BlockSpec((rows // steps, features), lambda i, s: (jnp.minimum(i, steps - 1), 0)),
                pl.BlockSpec((hidden, features), lambda i, s: (0, 0)),
                tile,
            ],
            out_specs=tile,
            scratch_shapes=[pltpu.VMEM((8, rows), jnp.int32), pltpu.VMEM((rows, hidden), jnp.bfloat16)],
        ),
        out_shape=jax.ShapeDtypeStruct((4 * share, hidden), jnp.bfloat16),
        input_output_aliases={4: 0},
        name="late",
        cost_estimate=pl.CostEstimate(
            flops=2 * rows * hidden * (features + share * count),
            bytes_accessed=2 * features * (rows + hidden) + 4 * share * count * hidden,
            transcendentals=0,
        ),
        compiler_params=pltpu.CompilerParams(vmem_limit_bytes=56 << 20),
    )(order, x, x, weight, old)


def hold_kernel(a_ref, o_ref):
    o_ref[...] = a_ref[...]


def hold(a):
    a = a[:8, :128]
    return pl.pallas_call(
        hold_kernel,
        out_shape=jax.ShapeDtypeStruct(a.shape, a.dtype),
        compiler_params=pltpu.CompilerParams(has_side_effects=True),
    )(a)


def shards(cotangent, slot_token, slot_gate, w_down):
    tokens, features = cotangent.shape
    experts, width = slot_token.shape[1:]
    half = experts // 2
    mid = tokens // 2
    share = 2 * tokens
    weight = w_down[0]
    zhi = lax.axis_index("zhi")
    z = zhi * 4 + lax.axis_index("zlo")

    def send(number, parts):
        scaled = dispatch(number, zhi, parts, half, width)
        return scaled, lax.all_to_all(scaled, PLANE, split_axis=0, concat_axis=0, tiled=True)

    own = jnp.concatenate([cotangent, pack_table(slot_token, slot_gate, features)], axis=0)
    u1, d1 = ring(own, own)
    _, x0 = send(0, [own])
    u2, d2 = ring(u1, d1)
    _, x1 = send(1, [u1, d1])
    hold(x0)
    u3, d3 = ring(u2, d2)
    _, x2 = send(2, [u2, d2])
    hold(x1)
    u4, d4 = ring(u3[mid:], d3[:mid])
    _, x3 = send(3, [u3, d3, u4, d4])

    out = early(z, x0, x1, x2, weight, half, width, share)
    out = late(z, x3, weight, out, half, width, share)
    return out[None]


def solution(mesh):
    fine = Mesh(mesh.devices.reshape(2, 4, 4, 2, 4), AXES)
    wide = ("zhi", "y", "x", "core")
    in_specs = (P(AXES, None), P(AXES, None, None), P(AXES, None, None), P(wide, "zlo", None))
    return jax.shard_map(shards, mesh=fine, in_specs=in_specs, out_specs=P(wide, None, "zlo"), check_vma=False)
```

time: 264 us -> 238 us (0.902)
  matrix products: 88.1 us -> 0 us
  Pallas kernels: 0 us -> 78.9 us
  blocking collectives: 24.4 us -> 0 us
  starting transfers between devices: 32.8 us -> 47.6 us
  between operations: 13.3 us -> 0.19 us
    dot_general x9 -> x0, matrix products: 88.1 us -> none  [the longest x4 38.3 us: shards(): picked = jnp.dot(pick, part, preferred_element_type=jnp.float32)]
    ppermute x0 -> x8, waiting for transfers between devices: none -> 82.6 us  [ring(): return (lax.ppermute(a, COLUMN, UP), lax.ppermute(b, COLUMN, DOWN))]
    pallas_call x0 -> x8, Pallas kernels: none -> 78.9 us  [the longest x4 31.1 us: dispatch(): pl.pallas_call(functools.partial(dispatch_kernel, len(sources), pieces, h...]
    all_gather x4 -> x0, waiting for transfers between devices: 67.8 us -> none  [shards(): lax.all_gather(cotangent[:, start:start + chunk], COLUMN, axis=0, tiled=T...]
    all_gather x1 -> x0, blocking collectives: 24.4 us -> none  [shards(): lax.all_gather(table, COLUMN, axis=0, tiled=True)]
    ppermute x0 -> x8, starting transfers between devices: none -> 14.2 us  [ring(): return (lax.ppermute(a, COLUMN, UP), lax.ppermute(b, COLUMN, DOWN))]
    all_to_all x4, waiting for transfers between devices: 25.2 us -> 14.8 us  [send(): lax.all_to_all(scaled, PLANE, split_axis=0, concat_axis=0, tiled=True)]
  transfers between devices with their start and end apart: 8 -> 12, of which waited for: 8 -> 6; matrix products, arithmetic and copies ran while one was open for 25% -> 1% of each run, Pallas kernels for 0% -> 25%
where the time goes in v2:
time: 238 us; the launch traced here: 235 us
  waiting for transfers between devices  97.4 us (41%)
  Pallas kernels  78.9 us (33%)
  starting transfers between devices  47.6 us (20%)
  local copies, waits for them, and re-layouts  7.46 us (3%)
  other arithmetic  3.73 us (2%)
    ppermute x8, waiting for transfers between devices, ring(): return (lax.ppermute(a, COLUMN, UP), lax.ppermute(b, COLUMN, DOWN))  82.6 us
    all_to_all x4, starting transfers between devices, send(): lax.all_to_all(scaled, PLANE, split_axis=0, concat_axis=0, tiled=True)  33.4 us
    pallas_call x4, Pallas kernels, dispatch(): pl.pallas_call(functools.partial(dispatch_kernel, len(sources), pieces, h...  31.1 us
    pallas_call x1, Pallas kernels, early(): pl.pallas_call(functools.partial(early_kernel, half, width), grid_spec=pl...  30.2 us
    pallas_call x1, Pallas kernels, late(): pl.pallas_call(functools.partial(late_kernel, half, width, steps), grid_s...  15.2 us
    all_to_all x4, waiting for transfers between devices, send(): lax.all_to_all(scaled, PLANE, split_axis=0, concat_axis=0, tiled=True)  14.8 us
    ppermute x8, starting transfers between devices, ring(): return (lax.ppermute(a, COLUMN, UP), lax.ppermute(b, COLUMN, DOWN))  14.2 us
  transfers between devices with their start and end apart: 12, of which 6 were waited for; matrix products, arithmetic and copies ran while one was open for 1% of the time, Pallas kernels for 25%

profile of v2, /device:TPU:1, one launch (start us, length us, event | category | flops | bytes accessed | tf_op | source)
XLA Modules:
  0.0 235.2 jit_solution(16274289244001782500)
XLA Ops:
  0.0 0.8 copy.9
  0.8 0.1 reshape.67
  0.9 0.7 convert_convert_fusion
  1.6 0.1 copy.8
  1.7 0.2 reshape.66
  1.9 2.3 pad_maximum_fusion.refs_0_
  4.3 0.0 copy-start
  4.3 5.5 %shard_map.46 = bf16[1280,512]{1,0:T(8,128)(2,1)} custom-call(s32[1]{0:T(128)} %bitcast.zhi_ref, bf16[264,2048]{1,0:T(8,128)(2,1)} %pad_maximum_fusion.refs_0_), custom_call_target="tpu_custom_call" | custom-call | flops 346030080 | bytes 2392064 | tf_op jit(solution)/shard_map/pallas_call | solution.py:96
  9.7 8.6 %all-to-all-start = ((bf16[32,40,512]{2,1,0:T(8,128)(2,1)}), bf16[32,40,512]{2,1,0:T(8,128)(2,1)S(1)}, u32[]{:S(2)}, u32[]{:S(2)}) async-start(bf16[32,40,512]{2,1,0:T(8,128)(2,1)} %bitcast.19), calls=%async_computation | async-start | bytes 2621440 | tf_op jit(solution)/shard_map/all_to_all | solution.py:283
  18.3 0.0 copy-done
  18.3 1.7 collective-permute-start
  20.0 4.0 %collective-permute-start.1 = (bf16[264,2048]{1,0:T(8,128)(2,1)S(1)}, bf16[264,2048]{1,0:T(8,128)(2,1)}, u32[]{:S(2)}, u32[]{:S(2)}) collective-permute-start(bf16[264,2048]{1,0:T(8,128)(2,1)S(1)} %copy-done), channel_id=1, source_target_pairs={{0,131},{1,0},{2,1},{3,2},{128,3},{129,128},{130,129},{131,130},{4... | collective-permute-start | bytes 3244040 | tf_op jit(solution)/shard_map/ppermute | solution.py:26
  24.1 23.9 %collective-permute-done.refs_0_ = bf16[264,2048]{1,0:T(8,128)(2,1)S(1)} collective-permute-done((bf16[264,2048]{1,0:T(8,128)(2,1)S(1)}, bf16[264,2048]{1,0:T(8,128)(2,1)S(1)}, u32[]{:S(2)}, u32[]{:S(2)}) %collective-permute-start) | collective-permute-done | bytes 1081376 | tf_op jit(solution)/shard_map/ppermute | solution.py:26
  48.0 0.0 copy-start.5
  48.0 1.0 copy-done.5
  49.0 0.0 collective-permute-done.1.refs_1_
  49.0 7.3 %shard_map.48 = bf16[1280,1024]{1,0:T(8,128)(2,1)} custom-call(s32[1]{0:T(128)} %bitcast.zhi_ref, bf16[264,2048]{1,0:T(8,128)(2,1)} %copy-done.5, bf16[264,2048]{1,0:T(8,128)(2,1)} %collective-permute-done.1.refs_1_), custom_call_target="tpu_custom_call" | custom-call | flops 1384120320 | bytes 4784128 | tf_op jit(solution)/shard_map/pallas_call | solution.py:96
  56.3 0.0 all-to-all-done
  56.3 0.0 copy-start.2
  56.3 1.1 copy-done.2
  57.4 7.8 %all-to-all-start.1 = ((bf16[32,40,1024]{2,1,0:T(8,128)(2,1)}), bf16[32,40,1024]{2,1,0:T(8,128)(2,1)S(1)}, u32[]{:S(2)}, u32[]{:S(2)}) async-start(bf16[32,40,1024]{2,1,0:T(8,128)(2,1)} %bitcast.24), calls=%async_computation.1 | async-start | bytes 5242880 | tf_op jit(solution)/shard_map/all_to_all | solution.py:283
  65.2 0.1 collective-permute-start.2
  65.3 2.7 %collective-permute-start.4 = (bf16[264,2048]{1,0:T(8,128)(2,1)}, bf16[264,2048]{1,0:T(8,128)(2,1)}, u32[]{:S(2)}, u32[]{:S(2)}) collective-permute-start(bf16[264,2048]{1,0:T(8,128)(2,1)} %collective-permute-done.1.refs_1_), channel_id=1, source_target_pairs={{0,131},{1,0},{2,1},{3,2},{128,3},{129,128},{130,129},{131,130},{4... | collective-permute-start | bytes 3244040 | tf_op jit(solution)/shard_map/ppermute | solution.py:26
  68.0 24.0 %collective-permute-done.2.refs_0_ = bf16[264,2048]{1,0:T(8,128)(2,1)} collective-permute-done((bf16[264,2048]{1,0:T(8,128)(2,1)}, bf16[264,2048]{1,0:T(8,128)(2,1)}, u32[]{:S(2)}, u32[]{:S(2)}) %collective-permute-start.2) | collective-permute-done | bytes 1081376 | tf_op jit(solution)/shard_map/ppermute | solution.py:26
  92.0 0.0 collective-permute-done.4.refs_1_
  92.0 7.3 %shard_map.51 = bf16[1280,1024]{1,0:T(8,128)(2,1)} custom-call(s32[1]{0:T(128)} %bitcast.zhi_ref, bf16[264,2048]{1,0:T(8,128)(2,1)} %collective-permute-done.2.refs_0_, bf16[264,2048]{1,0:T(8,128)(2,1)} %collective-permute-done.4.refs_1_), custom_call_target="tpu_custom_call" | custom-call | flops 1384120320 | bytes 4784128 | tf_op jit(solution)/shard_map/pallas_call | solution.py:96
  99.3 0.0 all-to-all-done.1
  99.3 0.0 copy-start.1
  99.3 8.1 %all-to-all-start.3 = ((bf16[32,40,1024]{2,1,0:T(8,128)(2,1)}), bf16[32,40,1024]{2,1,0:T(8,128)(2,1)}, u32[]{:S(2)}, u32[]{:S(2)}) async-start(bf16[32,40,1024]{2,1,0:T(8,128)(2,1)} %bitcast.23), calls=%async_computation.3 | async-start | bytes 5242880 | tf_op jit(solution)/shard_map/all_to_all | solution.py:283
  107.5 1.3 collective-permute-start.3
  108.8 1.5 collective-permute-start.5
  110.3 23.9 %collective-permute-done.3.refs_0_ = bf16[264,2048]{1,0:T(8,128)(2,1)S(1)} collective-permute-done((bf16[264,2048]{1,0:T(8,128)(2,1)}, bf16[264,2048]{1,0:T(8,128)(2,1)S(1)}, u32[]{:S(2)}, u32[]{:S(2)}) %collective-permute-start.3) | collective-permute-done | bytes 1081376 | tf_op jit(solution)/shard_map/ppermute | solution.py:26
  134.2 0.0 copy-start.3
  134.2 0.1 collective-permute-start.6
  134.4 0.0 collective-permute-done.5.refs_1_
  134.4 0.0 copy-start.4
  134.4 2.7 %collective-permute-start.7 = (bf16[128,2048]{1,0:T(8,128)(2,1)S(1)}, bf16[128,2048]{1,0:T(8,128)(2,1)S(1)}, u32[]{:S(2)}, u32[]{:S(2)}) collective-permute-start(bf16[128,2048]{1,0:T(8,128)(2,1)S(1)} %slice.19), channel_id=1, source_target_pairs={{0,131},{1,0},{2,1},{3,2},{128,3},{129,128},{130,129},{131,130},{4... | collective-permute-start | bytes 1572872 | tf_op jit(solution)/shard_map/ppermute | solution.py:26
  137.1 10.6 %collective-permute-done.7.refs_3_ = bf16[128,2048]{1,0:T(8,128)(2,1)S(1)} collective-permute-done((bf16[128,2048]{1,0:T(8,128)(2,1)S(1)}, bf16[128,2048]{1,0:T(8,128)(2,1)S(1)}, u32[]{:S(2)}, u32[]{:S(2)}) %collective-permute-start.7) | collective-permute-done | bytes 524320 | tf_op jit(solution)/shard_map/ppermute | solution.py:26
  147.7 0.0 copy-done.3
  147.7 0.0 copy-done.4
  147.7 0.0 copy-start.7
  147.7 0.8 copy-done.7
  148.5 0.2 collective-permute-done.6.refs_2_
  148.7 0.0 copy-start.6
  148.7 0.8 copy-done.6
  149.5 11.0 %shard_map.50 = bf16[1024,2048]{1,0:T(8,128)(2,1)} custom-call(s32[1]{0:T(128)} %bitcast.zhi_ref, bf16[264,2048]{1,0:T(8,128)(2,1)} %copy-done.3, bf16[264,2048]{1,0:T(8,128)(2,1)} %copy-done.4, bf16[136,2048]{1,0:T(8,128)(2,1)} %copy-done.6, bf16[128,2048]{1,0:T(8,128)(2,1)} %copy-done.7), custom_call_target="tpu_custom_call" | custom-call | flops 3321888768 | bytes 7438336 | tf_op jit(solution)/shard_map/pallas_call | solution.py:96
  160.5 0.0 all-to-all-done.3
  160.5 8.9 %all-to-all-start.2 = ((bf16[32,32,2048]{2,1,0:T(8,128)(2,1)}), bf16[32,32,2048]{2,1,0:T(8,128)(2,1)}, u32[]{:S(2)}, u32[]{:S(2)}) async-start(bf16[32,32,2048]{2,1,0:T(8,128)(2,1)} %bitcast.20), calls=%async_computation.2 | async-start | bytes 8388608 | tf_op jit(solution)/shard_map/all_to_all | solution.py:283
  169.4 0.7 stack.40.s_ref
  170.1 0.7 pad_add_fusion.s_ref
  170.8 1.3 slice.16.a_ref
  172.0 1.2 shard_map.47
  173.2 0.0 copy-done.1
  173.2 0.6 slice.17.a_ref
  173.8 1.2 shard_map.49
  175.0 30.2 %early.1.old_ref = bf16[2048,1024]{1,0:T(8,128)(2,1)} custom-call(s32[5]{0:T(128)} %stack.40.s_ref, bf16[1280,512]{1,0:T(8,128)(2,1)} %bitcast.26, bf16[1280,1024]{1,0:T(8,128)(2,1)} %bitcast.22, bf16[1280,1024]{1,0:T(8,128)(2,1)} %bitcast.17.x2_ref, bf16[1024,2048]{1,0:T(8,128)(2,1)} %bitcast.27), custom_call_target="tpu_custom_call" | custom-call | flops 19327352832 | bytes 18874368 | tf_op jit(solution)/shard_map/early/pallas_call | solution.py:181
  205.2 14.8 %all-to-all-done.2 = bf16[32,32,2048]{2,1,0:T(8,128)(2,1)} async-done(((bf16[32,32,2048]{2,1,0:T(8,128)(2,1)}), bf16[32,32,2048]{2,1,0:T(8,128)(2,1)}, u32[]{:S(2)}, u32[]{:S(2)}) %all-to-all-start.2) | async-done | bytes 4194336 | tf_op jit(solution)/shard_map/all_to_all | solution.py:283
  220.0 15.2 %late.1 = bf16[2048,1024]{1,0:T(8,128)(2,1)} custom-call(s32[4]{0:T(128)} %pad_add_fusion.s_ref, bf16[1024,2048]{1,0:T(8,128)(2,1)} %bitcast.10.front_ref.x_ref, bf16[1024,2048]{1,0:T(8,128)(2,1)} %bitcast.10.front_ref.x_ref, bf16[1024,2048]{1,0:T(8,128)(2,1)} %bitcast.28, bf16[2048,1024]{1,0:T(8,128)(2,1)} %early.1.old_ref), custom_call_target="tpu_custom_call", output_to_operand_aliasing={{}: (4, {})} | custom-call | flops 7516192768 | bytes 14680064 | tf_op jit(solution)/shard_map/late/pallas_call | solution.py:232
  (4 shorter events, 0.1 us)
Async XLA Ops:
  4.3 14.1 %copy-start = (bf16[264,2048]{1,0:T(8,128)(2,1)S(1)}, bf16[264,2048]{1,0:T(8,128)(2,1)}, u32[]{:S(2)}) copy-start(bf16[264,2048]{1,0:T(8,128)(2,1)} %pad_maximum_fusion.refs_0_) | copy-start | bytes 3244036
  9.7 46.6 %all-to-all-start = ((bf16[32,40,512]{2,1,0:T(8,128)(2,1)}), bf16[32,40,512]{2,1,0:T(8,128)(2,1)S(1)}, u32[]{:S(2)}, u32[]{:S(2)}) async-start(bf16[32,40,512]{2,1,0:T(8,128)(2,1)} %bitcast.19), calls=%async_computation | async-start | bytes 2621440 | tf_op jit(solution)/shard_map/all_to_all | solution.py:283
  18.3 29.7 %collective-permute-start = (bf16[264,2048]{1,0:T(8,128)(2,1)S(1)}, bf16[264,2048]{1,0:T(8,128)(2,1)S(1)}, u32[]{:S(2)}, u32[]{:S(2)}) collective-permute-start(bf16[264,2048]{1,0:T(8,128)(2,1)S(1)} %copy-done), channel_id=1, source_target_pairs={{0,1},{1,2},{2,3},{3,128},{128,129},{129,130},{130,131},{131,0},{4... | collective-permute-start | bytes 3244040 | tf_op jit(solution)/shard_map/ppermute | solution.py:26
  20.0 29.0 %collective-permute-start.1 = (bf16[264,2048]{1,0:T(8,128)(2,1)S(1)}, bf16[264,2048]{1,0:T(8,128)(2,1)}, u32[]{:S(2)}, u32[]{:S(2)}) collective-permute-start(bf16[264,2048]{1,0:T(8,128)(2,1)S(1)} %copy-done), channel_id=1, source_target_pairs={{0,131},{1,0},{2,1},{3,2},{128,3},{129,128},{130,129},{131,130},{4... | collective-permute-start | bytes 3244040 | tf_op jit(solution)/shard_map/ppermute | solution.py:26
  48.0 1.0 copy-start.5
  56.3 1.1 copy-start.2
  57.4 41.9 %all-to-all-start.1 = ((bf16[32,40,1024]{2,1,0:T(8,128)(2,1)}), bf16[32,40,1024]{2,1,0:T(8,128)(2,1)S(1)}, u32[]{:S(2)}, u32[]{:S(2)}) async-start(bf16[32,40,1024]{2,1,0:T(8,128)(2,1)} %bitcast.24), calls=%async_computation.1 | async-start | bytes 5242880 | tf_op jit(solution)/shard_map/all_to_all | solution.py:283
  65.2 26.8 %collective-permute-start.2 = (bf16[264,2048]{1,0:T(8,128)(2,1)}, bf16[264,2048]{1,0:T(8,128)(2,1)}, u32[]{:S(2)}, u32[]{:S(2)}) collective-permute-start(bf16[264,2048]{1,0:T(8,128)(2,1)} %copy-done.5), channel_id=1, source_target_pairs={{0,1},{1,2},{2,3},{3,128},{128,129},{129,130},{130,131},{131,0},{4... | collective-permute-start | bytes 3244040 | tf_op jit(solution)/shard_map/ppermute | solution.py:26
  65.3 26.7 %collective-permute-start.4 = (bf16[264,2048]{1,0:T(8,128)(2,1)}, bf16[264,2048]{1,0:T(8,128)(2,1)}, u32[]{:S(2)}, u32[]{:S(2)}) collective-permute-start(bf16[264,2048]{1,0:T(8,128)(2,1)} %collective-permute-done.1.refs_1_), channel_id=1, source_target_pairs={{0,131},{1,0},{2,1},{3,2},{128,3},{129,128},{130,129},{131,130},{4... | collective-permute-start | bytes 3244040 | tf_op jit(solution)/shard_map/ppermute | solution.py:26
  99.3 73.9 %copy-start.1 = (bf16[32,40,1024]{2,1,0:T(8,128)(2,1)}, bf16[32,40,1024]{2,1,0:T(8,128)(2,1)S(1)}, u32[]{:S(2)}) copy-start(bf16[32,40,1024]{2,1,0:T(8,128)(2,1)S(1)} %all-to-all-done.1) | copy-start | bytes 7864324
  99.3 61.1 %all-to-all-start.3 = ((bf16[32,40,1024]{2,1,0:T(8,128)(2,1)}), bf16[32,40,1024]{2,1,0:T(8,128)(2,1)}, u32[]{:S(2)}, u32[]{:S(2)}) async-start(bf16[32,40,1024]{2,1,0:T(8,128)(2,1)} %bitcast.23), calls=%async_computation.3 | async-start | bytes 5242880 | tf_op jit(solution)/shard_map/all_to_all | solution.py:283
  107.5 26.7 %collective-permute-start.3 = (bf16[264,2048]{1,0:T(8,128)(2,1)}, bf16[264,2048]{1,0:T(8,128)(2,1)S(1)}, u32[]{:S(2)}, u32[]{:S(2)}) collective-permute-start(bf16[264,2048]{1,0:T(8,128)(2,1)} %collective-permute-done.2.refs_0_), channel_id=1, source_target_pairs={{0,1},{1,2},{2,3},{3,128},{128,129},{129,130},{130,131},{131,0},{4... | collective-permute-start | bytes 3244040 | tf_op jit(solution)/shard_map/ppermute | solution.py:26
  108.8 25.6 %collective-permute-start.5 = (bf16[264,2048]{1,0:T(8,128)(2,1)}, bf16[264,2048]{1,0:T(8,128)(2,1)S(1)}, u32[]{:S(2)}, u32[]{:S(2)}) collective-permute-start(bf16[264,2048]{1,0:T(8,128)(2,1)} %collective-permute-done.4.refs_1_), channel_id=1, source_target_pairs={{0,131},{1,0},{2,1},{3,2},{128,3},{129,128},{130,129},{131,130},{4... | collective-permute-start | bytes 3244040 | tf_op jit(solution)/shard_map/ppermute | solution.py:26
  134.2 13.5 %copy-start.3 = (bf16[264,2048]{1,0:T(8,128)(2,1)}, bf16[264,2048]{1,0:T(8,128)(2,1)S(1)}, u32[]{:S(2)}) copy-start(bf16[264,2048]{1,0:T(8,128)(2,1)S(1)} %collective-permute-done.3.refs_0_) | copy-start | bytes 3244036
  134.2 14.4 %collective-permute-start.6 = (bf16[136,2048]{1,0:T(8,128)(2,1)S(1)}, bf16[136,2048]{1,0:T(8,128)(2,1)S(1)}, u32[]{:S(2)}, u32[]{:S(2)}) collective-permute-start(bf16[136,2048]{1,0:T(8,128)(2,1)S(1)} %slice.18), channel_id=1, source_target_pairs={{0,1},{1,2},{2,3},{3,128},{128,129},{129,130},{130,131},{131,0},{4... | collective-permute-start | bytes 1671176 | tf_op jit(solution)/shard_map/ppermute | solution.py:26
  134.4 13.3 %copy-start.4 = (bf16[264,2048]{1,0:T(8,128)(2,1)}, bf16[264,2048]{1,0:T(8,128)(2,1)S(1)}, u32[]{:S(2)}) copy-start(bf16[264,2048]{1,0:T(8,128)(2,1)S(1)} %collective-permute-done.5.refs_1_) | copy-start | bytes 3244036
  134.4 13.3 %collective-permute-start.7 = (bf16[128,2048]{1,0:T(8,128)(2,1)S(1)}, bf16[128,2048]{1,0:T(8,128)(2,1)S(1)}, u32[]{:S(2)}, u32[]{:S(2)}) collective-permute-start(bf16[128,2048]{1,0:T(8,128)(2,1)S(1)} %slice.19), channel_id=1, source_target_pairs={{0,131},{1,0},{2,1},{3,2},{128,3},{129,128},{130,129},{131,130},{4... | collective-permute-start | bytes 1572872 | tf_op jit(solution)/shard_map/ppermute | solution.py:26
  147.7 0.8 copy-start.7
  148.7 0.8 copy-start.6
  160.5 59.6 %all-to-all-start.2 = ((bf16[32,32,2048]{2,1,0:T(8,128)(2,1)}), bf16[32,32,2048]{2,1,0:T(8,128)(2,1)}, u32[]{:S(2)}, u32[]{:S(2)}) async-start(bf16[32,32,2048]{2,1,0:T(8,128)(2,1)} %bitcast.20), calls=%async_computation.2 | async-start | bytes 8388608 | tf_op jit(solution)/shard_map/all_to_all | solution.py:283

commit v3 on v2

v3 whole, which is shorter than its diff:
```python
import functools

import jax
import jax.numpy as jnp
from jax import lax
from jax.experimental import pallas as pl
from jax.experimental.pallas import tpu as pltpu
from jax.sharding import Mesh, PartitionSpec as P


AXES = ("zhi", "y", "x", "core", "zlo")
COLUMN = ("zhi", "zlo")
PLANE = ("y", "x", "core")
PLANES = 8
DEAD = 128.0
HEAD = 8
UP = [(i, (i + 1) % PLANES) for i in range(PLANES)]
SWAP = [(i, i ^ 1) for i in range(PLANES)]
DOWN = [(i, (i - 1) % PLANES) for i in range(PLANES)]
GROUPS = ((1, 4), (1, 4), (2, 2), (3, 1))
TILES = 4
SKIP = 8192
CONTRACT_LAST = (((1,), (1,)), ((), ()))


def ring(a, b):
    return lax.ppermute(a, COLUMN, UP), lax.ppermute(b, COLUMN, DOWN)


def pack_table(slot_token, slot_gate, columns):
    gate = slot_gate.reshape(1, -1)
    high = lax.reduce_precision(gate, 8, 7)
    middle = lax.reduce_precision(gate - high, 8, 7)
    low = gate - high - middle
    table = jnp.concatenate([slot_token.astype(jnp.float32).reshape(1, -1), high, middle, low], axis=0)
    return jnp.pad(table, ((0, HEAD - 4), (0, columns - table.shape[1]))).astype(jnp.bfloat16)


def dispatch_kernel(number, half, width, padded, s_ref, *refs):
    *parts, out_ref, stack_ref, table_ref = refs
    sources, pieces = GROUPS[number]
    columns = out_ref.shape[1]
    each = half // TILES
    rows = each * padded
    depth = stack_ref.shape[0]
    tokens = depth // (sources * pieces)
    slots = table_ref.shape[2]
    t = pl.program_id(0)

    def load(j, ref, base, length, table=True):
        for q in range(pieces):
            to = (j * pieces + q) * tokens + base
            stack_ref[to : to + length, :] = ref[:length, q * columns : (q + 1) * columns]
        if table:
            table_ref[j] = ref[length : length + HEAD, :slots]

    if number == 1:
        pl.when((t == 0) & (s_ref[1] == 0))(functools.partial(load, 0, parts[0], 0, tokens))
        pl.when((t == 0) & (s_ref[1] == 1))(functools.partial(load, 0, parts[1], 0, tokens))
    else:

        @pl.when(t == 0)
        def _():
            for j in range(min(sources, 2)):
                load(j, parts[j], 0, tokens)
            if number == 3:
                mid = tokens // 2
                load(2, parts[2], mid, mid)
                load(2, parts[3], 0, mid, table=False)

    first = s_ref[0] * half + t * each
    index = lax.broadcasted_iota(jnp.int32, (rows, 1), 0).astype(jnp.float32)
    place = jnp.floor((index + 0.5) * (1.0 / padded))
    rem = index - place * padded
    block = jnp.floor((rem + 0.5) * (1.0 / width))
    target = (first.astype(jnp.float32) + place) * width + rem - block * width
    lane = lax.broadcasted_iota(jnp.int32, (rows, slots), 1)
    data = jnp.zeros((rows, HEAD), jnp.float32)
    for j in range(sources):
        mine = (block >= j * pieces) & (block < (j + 1) * pieces)
        mine = jnp.where(mine, target, -1.0).astype(jnp.int32)
        mine = jnp.where(lane == mine, 1.0, 0.0).astype(jnp.bfloat16)
        data = data + lax.dot_general(mine, table_ref[j], CONTRACT_LAST, preferred_element_type=jnp.float32)
    token = data[:, 0:1]
    gate = data[:, 1:2] + data[:, 2:3] + data[:, 3:4]
    goal = jnp.where((token >= 0.0) & (block < sources * pieces), token + block * tokens, -1.0).astype(jnp.int32)
    lane = lax.broadcasted_iota(jnp.int32, (rows, depth), 1)
    pick = jnp.where(lane == goal, 1.0, 0.0).astype(jnp.bfloat16)
    total = jnp.dot(pick, stack_ref[...], preferred_element_type=jnp.float32)
    out_ref[...] = jnp.where(goal >= 0, gate * total, DEAD).astype(jnp.bfloat16)


def dispatch(number, scalars, parts, tokens, half, width):
    sources, pieces = GROUPS[number]
    columns = parts[0].shape[1] // pieces
    used = sources * pieces * width
    padded = -(-used // 8) * 8
    rows = half * padded
    depth = sources * pieces * tokens
    return pl.pallas_call(
        functools.partial(dispatch_kernel, number, half, width, padded),
        grid_spec=pltpu.PrefetchScalarGridSpec(
            num_scalar_prefetch=1,
            grid=(TILES,),
            in_specs=[pl.BlockSpec(p.shape, lambda t, s: (0, 0)) for p in parts],
            out_specs=pl.BlockSpec((rows // TILES, columns), lambda t, s: (t, 0)),
            scratch_shapes=[
                pltpu.VMEM((depth, columns), jnp.bfloat16),
                pltpu.VMEM((sources, HEAD, 2 * half * width), jnp.bfloat16),
            ],
        ),
        out_shape=jax.ShapeDtypeStruct((rows, columns), jnp.bfloat16),
        cost_estimate=pl.CostEstimate(
            flops=2 * rows * depth * columns, bytes_accessed=2 * (depth + rows) * columns, transcendentals=0
        ),
    )(scalars, *parts)


def places(x_ref, sources, pieces, half, width, share):
    rows = x_ref.shape[0]
    padded = rows // half
    first = jnp.where(lax.broadcasted_iota(jnp.int32, (8, 128), 1) == 0, 1.0, 0.0).astype(jnp.bfloat16)
    value = lax.dot_general(first, x_ref[:, :128], CONTRACT_LAST, preferred_element_type=jnp.float32)

    def split(index, length):
        outer = jnp.floor((index + 0.5) * (1.0 / length))
        return outer, index - outer * length

    def parts(shape, axis):
        place, rem = split(lax.broadcasted_iota(jnp.int32, shape, axis).astype(jnp.float32), padded)
        block, slot = split(rem, width)
        source, piece = split(block, pieces)
        return place, block, slot, source, piece

    place, block, slot, source, piece = parts((1, rows), 1)
    alive = jnp.where((value < 64.0) & (block < len(sources) * pieces), 1.0, 0.0)
    place_down, _, _, source_down, piece_down = parts((rows, 1), 0)
    lane = lax.broadcasted_iota(jnp.int32, (rows, 128), 1)
    own = jnp.where(piece_down == 0.0, source_down * half + place_down, -1.0).astype(jnp.int32)
    own = jnp.where(lane == own, 1.0, 0.0).astype(jnp.bfloat16)
    count = jnp.dot(alive.astype(jnp.bfloat16), own, preferred_element_type=jnp.float32)
    of, at = split(lax.broadcasted_iota(jnp.int32, (128, 1), 0).astype(jnp.float32), half)
    ahead = jnp.where((of == source) & (at < place), 1.0, 0.0).astype(jnp.bfloat16)
    code = jnp.dot(count.astype(jnp.bfloat16), ahead, preferred_element_type=jnp.float32)
    code = code + slot + piece * float(SKIP)
    of, _ = split(lax.broadcasted_iota(jnp.int32, (1, 128), 1).astype(jnp.float32), half)
    for j, z in enumerate(sources):
        held = jnp.sum(jnp.where(of == j, count[0:1], 0.0), axis=1, keepdims=True)
        upper = jnp.where(z >= 4, 1.0, 0.0)
        base = (lax.rem(z, 4) * share).astype(jnp.float32) + upper * (share - held)
        code = code + jnp.where(source == j, base, 0.0)
    return jnp.where(alive > 0.0, code, -1.0).astype(jnp.int32)


def chosen(code, share, h, q):
    position = lax.broadcasted_iota(jnp.int32, (share, code.shape[1]), 0) + (h * share + SKIP * q)
    return jnp.where(code == position, 1.0, 0.0).astype(jnp.bfloat16)


def early_kernel(half, width, s_ref, x0_ref, xp_ref, x1_ref, x2_ref, w_ref, out_ref, row_ref, c_ref):
    i = pl.program_id(0)
    share = out_ref.shape[0]
    h = s_ref[i]

    def route(x_ref, sources, pieces):
        c_ref[...] = places(x_ref, sources, pieces, half, width, share)
        columns = x_ref.shape[1]
        for q in range(pieces):
            row_ref[:, q * columns : (q + 1) * columns] = jnp.dot(
                chosen(c_ref[0:1, :], share, h, q), x_ref[...], preferred_element_type=jnp.float32
            ).astype(jnp.bfloat16)

    for step, x_ref in enumerate((x0_ref, xp_ref, x1_ref)):
        pl.when(i == step)(functools.partial(route, x_ref, [s_ref[4 + step]], 4))
    pl.when(i == 3)(functools.partial(route, x2_ref, [s_ref[7], s_ref[8]], 2))

    out_ref[...] = lax.dot_general(
        row_ref[...], w_ref[...], CONTRACT_LAST, preferred_element_type=jnp.float32
    ).astype(jnp.bfloat16)


def early(sources, arrived, weight, half, width, share):
    hidden, features = weight.shape
    rows = arrived[0].shape[0]
    order = jnp.stack([s % 4 for s in sources[:4]] + sources)
    return pl.pallas_call(
        functools.partial(early_kernel, half, width),
        grid_spec=pltpu.PrefetchScalarGridSpec(
            num_scalar_prefetch=1,
            grid=(4,),
            in_specs=[pl.BlockSpec(a.shape, lambda i, s: (0, 0)) for a in (*arrived, weight)],
            out_specs=pl.BlockSpec((share, hidden), lambda i, s: (s[i], 0)),
            scratch_shapes=[
                pltpu.VMEM((share, features), jnp.bfloat16),
                pltpu.VMEM((8, rows), jnp.int32),
            ],
        ),
        out_shape=jax.ShapeDtypeStruct((4 * share, hidden), jnp.bfloat16),
        name="early",
        cost_estimate=pl.CostEstimate(
            flops=8 * share * features * (rows + hidden), bytes_accessed=4 * features * (rows + hidden), transcendentals=0
        ),
        compiler_params=pltpu.CompilerParams(vmem_limit_bytes=56 << 20),
    )(order, *arrived, weight)


def late_kernel(half, width, steps, s_ref, front_ref, x_ref, w_ref, old_ref, out_ref, c_ref, y_ref, p_ref):
    i = pl.program_id(0)
    share = out_ref.shape[0]
    tile = x_ref.shape[0]

    @pl.when(i == 0)
    def _():
        c_ref[...] = places(front_ref, [s_ref[3], s_ref[4], s_ref[5]], 1, half, width, share)

    def multiply():
        y_ref[pl.ds(pl.multiple_of(i * tile, 16), tile), :] = lax.dot_general(
            x_ref[...], w_ref[...], CONTRACT_LAST, preferred_element_type=jnp.float32
        ).astype(jnp.bfloat16)

    pl.when(i == 0)(multiply)

    @pl.when((i > 0) & (i < steps))
    def _():
        multiply()
        p_ref[i - 1] = chosen(c_ref[0:1, :], share, s_ref[i - 1], 0)

    @pl.when(i >= steps)
    def _():
        out = jnp.dot(p_ref[jnp.maximum(i - steps, 0)], y_ref[...], preferred_element_type=jnp.float32)
        out_ref[...] = (out + old_ref[...].astype(jnp.float32)).astype(jnp.bfloat16)


def late(sources, x, weight, old, half, width, share):
    hidden, features = weight.shape
    rows = x.shape[0]
    steps = 4
    order = jnp.stack([s % 4 for s in sources] + sources)
    count = len(sources)
    tile = pl.BlockSpec((share, hidden), lambda i, s: (s[jnp.maximum(i - steps, 0)], 0))
    return pl.pallas_call(
        functools.partial(late_kernel, half, width, steps),
        grid_spec=pltpu.PrefetchScalarGridSpec(
            num_scalar_prefetch=1,
            grid=(steps + count,),
            in_specs=[
                pl.BlockSpec((rows, 128), lambda i, s: (0, 0)),
                pl.BlockSpec((rows // steps, features), lambda i, s: (jnp.minimum(i, steps - 1), 0)),
                pl.BlockSpec((hidden, features), lambda i, s: (0, 0)),
                tile,
            ],
            out_specs=tile,
            scratch_shapes=[
                pltpu.VMEM((8, rows), jnp.int32),
                pltpu.VMEM((rows, hidden), jnp.bfloat16),
                pltpu.VMEM((count, share, rows), jnp.bfloat16),
            ],
        ),
        out_shape=jax.ShapeDtypeStruct((4 * share, hidden), jnp.bfloat16),
        input_output_aliases={4: 0},
        name="late",
        cost_estimate=pl.CostEstimate(
            flops=2 * rows * hidden * (features + share * count),
            bytes_accessed=2 * features * (rows + hidden) + 4 * share * count * hidden,
            transcendentals=0,
        ),
        compiler_params=pltpu.CompilerParams(vmem_limit_bytes=56 << 20),
    )(order, x, x, weight, old)


def hold_kernel(a_ref, o_ref):
    o_ref[...] = a_ref[...]


def hold(a):
    a = a[:8, :128]
    return pl.pallas_call(
        hold_kernel,
        out_shape=jax.ShapeDtypeStruct(a.shape, a.dtype),
        compiler_params=pltpu.CompilerParams(has_side_effects=True),
    )(a)


def shards(cotangent, slot_token, slot_gate, w_down):
    tokens, features = cotangent.shape
    experts, width = slot_token.shape[1:]
    half = experts // 2
    mid = tokens // 2
    share = 2 * tokens
    weight = w_down[0]
    zhi = lax.axis_index("zhi")
    z = zhi * 4 + lax.axis_index("zlo")
    odd = z % 2
    scalars = jnp.stack([zhi, odd])

    def send(number, parts):
        scaled = dispatch(number, scalars, parts, tokens, half, width)
        return scaled, lax.all_to_all(scaled, PLANE, split_axis=0, concat_axis=0, tiled=True)

    own = jnp.concatenate([cotangent, pack_table(slot_token, slot_gate, features)], axis=0)
    u1, d1 = ring(own, own)
    _, x0 = send(0, [own])
    u2, d2 = ring(u1, d1)
    _, x1 = send(1, [u1, d1])
    hold(x0)
    u3, d3 = ring(u2, d2)
    _, x2 = send(2, [u2, d2])
    hold(x1)
    u4, d4 = ring(u3[mid:], d3[:mid])
    _, x3 = send(3, [u3, d3, u4, d4])

    xp = lax.ppermute(x0, COLUMN, SWAP)

    def at(*offsets):
        return [(z + o) % PLANES for o in offsets]

    partner = z + 1 - 2 * odd
    other = (z - 1 + 2 * odd) % PLANES
    out = early([z, partner, other] + at(-2, 2), (x0, xp, x1, x2), weight, half, width, share)
    out = late(at(-3, 3, 4), x3, weight, out, half, width, share)
    return out[None]


def solution(mesh):
    fine = Mesh(mesh.devices.reshape(2, 4, 4, 2, 4), AXES)
    wide = ("zhi", "y", "x", "core")
    in_specs = (P(AXES, None), P(AXES, None, None), P(AXES, None, None), P(wide, "zlo", None))
    return jax.shard_map(shards, mesh=fine, in_specs=in_specs, out_specs=P(wide, None, "zlo"), check_vma=False)
```

time: 238 us -> 234 us (0.983)
  waiting for transfers between devices: 97.4 us -> 92.2 us
  local copies, waits for them, and re-layouts: 7.46 us -> 11.5 us
    ppermute x0 -> x1, waiting for transfers between devices: none -> 23.1 us  [shards(): xp = lax.ppermute(x0, COLUMN, SWAP)]
    ppermute x8, waiting for transfers between devices: 82.6 us -> 65.8 us  [ring(): return (lax.ppermute(a, COLUMN, UP), lax.ppermute(b, COLUMN, DOWN))]
    all_to_all x4, waiting for transfers between devices: 14.8 us -> 3.26 us  [send(): lax.all_to_all(scaled, PLANE, split_axis=0, concat_axis=0, tiled=True)]
    unnamed x17 -> x19, local copies, waits for them, and re-layouts: 4.49 us -> 7.26 us
  transfers between devices with their start and end apart: 12 -> 13, of which waited for: 6 -> 7; matrix products, arithmetic and copies ran while one was open for 1% -> 2% of each run, Pallas kernels for 25% -> 25%
where the time goes in v3:
time: 234 us; the launch traced here: 233 us
  waiting for transfers between devices  92.2 us (39%)
  Pallas kernels  78.6 us (34%)
  starting transfers between devices  46.7 us (20%)
  local copies, waits for them, and re-layouts  11.5 us (5%)
  other arithmetic  3.71 us (2%)
    ppermute x8, waiting for transfers between devices, ring(): return (lax.ppermute(a, COLUMN, UP), lax.ppermute(b, COLUMN, DOWN))  65.8 us
    all_to_all x4, starting transfers between devices, send(): lax.all_to_all(scaled, PLANE, split_axis=0, concat_axis=0, tiled=True)  31.4 us
    pallas_call x4, Pallas kernels, dispatch(): pl.pallas_call(functools.partial(dispatch_kernel, number, half, width, pa...  30.6 us
    pallas_call x1, Pallas kernels, early(): pl.pallas_call(functools.partial(early_kernel, half, width), grid_spec=pl...  30.1 us
    ppermute x1, waiting for transfers between devices, shards(): xp = lax.ppermute(x0, COLUMN, SWAP)  23.1 us
    pallas_call x1, Pallas kernels, late(): pl.pallas_call(functools.partial(late_kernel, half, width, steps), grid_s...  15.4 us
    ppermute x8, starting transfers between devices, ring(): return (lax.ppermute(a, COLUMN, UP), lax.ppermute(b, COLUMN, DOWN))  14.2 us
    unnamed x19, local copies, waits for them, and re-layouts  7.26 us
  transfers between devices with their start and end apart: 13, of which 7 were waited for; matrix products, arithmetic and copies ran while one was open for 2% of the time, Pallas kernels for 25%

profile of v3, /device:TPU:1, one launch (start us, length us, event | category | flops | bytes accessed | tf_op | source)
XLA Modules:
  0.0 232.8 jit_solution(5869326800260422695)
XLA Ops:
  0.0 0.8 copy.9
  0.8 0.1 reshape.60
  0.9 0.7 convert_convert_fusion
  1.6 0.1 copy.8
  1.7 0.2 reshape.59
  1.9 0.6 pad_add_fusion.s_ref
  2.5 2.4 %pad_maximum_fusion.refs_0_ = bf16[264,2048]{1,0:T(8,128)(2,1)} fusion(bf16[8,2048]{1,0:T(8,128)(2,1)S(1)} %fusion.8, bf16[256,2048]{1,0:T(8,128)(2,1)} %param.4), kind=kLoop, calls=%fused_computation | loop fusion | flops 2162688 | bytes 2162688 | tf_op jit(solution)/shard_map/concatenate | solution.py:300
  4.9 6.1 %shard_map.46 = bf16[1280,512]{1,0:T(8,128)(2,1)} custom-call(s32[2]{0:T(128)} %pad_add_fusion.s_ref, bf16[264,2048]{1,0:T(8,128)(2,1)} %pad_maximum_fusion.refs_0_), custom_call_target="tpu_custom_call" | custom-call | flops 1342177280 | bytes 2359296 | tf_op jit(solution)/shard_map/pallas_call | solution.py:100
  11.0 0.0 copy-start.3
  11.0 8.7 %all-to-all-start = ((bf16[32,40,512]{2,1,0:T(8,128)(2,1)}), bf16[32,40,512]{2,1,0:T(8,128)(2,1)S(1)}, u32[]{:S(2)}, u32[]{:S(2)}) async-start(bf16[32,40,512]{2,1,0:T(8,128)(2,1)} %bitcast.35), calls=%async_computation | async-start | bytes 2621440 | tf_op jit(solution)/shard_map/all_to_all | solution.py:298
  19.7 0.0 copy-done.3
  19.7 1.7 collective-permute-start
  21.4 4.0 %collective-permute-start.1 = (bf16[264,2048]{1,0:T(8,128)(2,1)S(1)}, bf16[264,2048]{1,0:T(8,128)(2,1)}, u32[]{:S(2)}, u32[]{:S(2)}) collective-permute-start(bf16[264,2048]{1,0:T(8,128)(2,1)S(1)} %copy-done.3), channel_id=1, source_target_pairs={{0,131},{1,0},{2,1},{3,2},{128,3},{129,128},{130,129},{131,130},{4... | collective-permute-start | bytes 3244040 | tf_op jit(solution)/shard_map/ppermute | solution.py:27
  25.5 24.0 %collective-permute-done.refs_0_ = bf16[264,2048]{1,0:T(8,128)(2,1)} collective-permute-done((bf16[264,2048]{1,0:T(8,128)(2,1)S(1)}, bf16[264,2048]{1,0:T(8,128)(2,1)}, u32[]{:S(2)}, u32[]{:S(2)}) %collective-permute-start) | collective-permute-done | bytes 1081376 | tf_op jit(solution)/shard_map/ppermute | solution.py:27
  49.5 0.0 collective-permute-start.2
  49.5 0.0 collective-permute-done.1.refs_1_
  49.5 2.7 %collective-permute-start.4 = (bf16[264,2048]{1,0:T(8,128)(2,1)}, bf16[264,2048]{1,0:T(8,128)(2,1)}, u32[]{:S(2)}, u32[]{:S(2)}) collective-permute-start(bf16[264,2048]{1,0:T(8,128)(2,1)} %collective-permute-done.1.refs_1_), channel_id=1, source_target_pairs={{0,131},{1,0},{2,1},{3,2},{128,3},{129,128},{130,129},{131,130},{4... | collective-permute-start | bytes 3244040 | tf_op jit(solution)/shard_map/ppermute | solution.py:27
  52.2 6.5 %shard_map.48 = bf16[1280,512]{1,0:T(8,128)(2,1)} custom-call(s32[2]{0:T(128)} %pad_add_fusion.s_ref, bf16[264,2048]{1,0:T(8,128)(2,1)} %collective-permute-done.refs_0_, bf16[264,2048]{1,0:T(8,128)(2,1)} %collective-permute-done.1.refs_1_), custom_call_target="tpu_custom_call" | custom-call | flops 1342177280 | bytes 2359296 | tf_op jit(solution)/shard_map/pallas_call | solution.py:100
  58.6 0.0 all-to-all-done
  58.6 0.0 copy-start.1
  58.6 1.1 copy-done.1
  59.7 8.3 %all-to-all-start.1 = ((bf16[32,40,512]{2,1,0:T(8,128)(2,1)}), bf16[32,40,512]{2,1,0:T(8,128)(2,1)S(1)}, u32[]{:S(2)}, u32[]{:S(2)}) async-start(bf16[32,40,512]{2,1,0:T(8,128)(2,1)} %bitcast.36), calls=%async_computation.1 | async-start | bytes 2621440 | tf_op jit(solution)/shard_map/all_to_all | solution.py:298
  68.0 7.6 %collective-permute-done.2.refs_0_ = bf16[264,2048]{1,0:T(8,128)(2,1)} collective-permute-done((bf16[264,2048]{1,0:T(8,128)(2,1)}, bf16[264,2048]{1,0:T(8,128)(2,1)}, u32[]{:S(2)}, u32[]{:S(2)}) %collective-permute-start.2) | collective-permute-done | bytes 1081376 | tf_op jit(solution)/shard_map/ppermute | solution.py:27
  75.6 0.0 collective-permute-done.4.refs_1_
  75.6 8.5 %shard_map.51 = bf16[1280,1024]{1,0:T(8,128)(2,1)} custom-call(s32[2]{0:T(128)} %pad_add_fusion.s_ref, bf16[264,2048]{1,0:T(8,128)(2,1)} %collective-permute-done.2.refs_0_, bf16[264,2048]{1,0:T(8,128)(2,1)} %collective-permute-done.4.refs_1_), custom_call_target="tpu_custom_call" | custom-call | flops 2684354560 | bytes 4718592 | tf_op jit(solution)/shard_map/pallas_call | solution.py:100
  84.1 3.3 %all-to-all-done.1 = bf16[32,40,512]{2,1,0:T(8,128)(2,1)S(1)} async-done(((bf16[32,40,512]{2,1,0:T(8,128)(2,1)}), bf16[32,40,512]{2,1,0:T(8,128)(2,1)S(1)}, u32[]{:S(2)}, u32[]{:S(2)}) %all-to-all-start.1) | async-done | bytes 1310752 | tf_op jit(solution)/shard_map/all_to_all | solution.py:298
  87.3 0.0 copy-start.2
  87.3 1.1 copy-done.2
  88.4 5.3 %all-to-all-start.3 = ((bf16[32,40,1024]{2,1,0:T(8,128)(2,1)}), bf16[32,40,1024]{2,1,0:T(8,128)(2,1)S(1)}, u32[]{:S(2)}, u32[]{:S(2)}) async-start(bf16[32,40,1024]{2,1,0:T(8,128)(2,1)} %bitcast.29), calls=%async_computation.3 | async-start | bytes 5242880 | tf_op jit(solution)/shard_map/all_to_all | solution.py:298
  93.7 0.1 collective-permute-start.3
  93.8 2.7 %collective-permute-start.5 = (bf16[264,2048]{1,0:T(8,128)(2,1)}, bf16[264,2048]{1,0:T(8,128)(2,1)S(1)}, u32[]{:S(2)}, u32[]{:S(2)}) collective-permute-start(bf16[264,2048]{1,0:T(8,128)(2,1)} %collective-permute-done.4.refs_1_), channel_id=1, source_target_pairs={{0,131},{1,0},{2,1},{3,2},{128,3},{129,128},{130,129},{131,130},{4... | collective-permute-start | bytes 3244040 | tf_op jit(solution)/shard_map/ppermute | solution.py:27
  96.6 23.8 %collective-permute-done.3.refs_0_ = bf16[264,2048]{1,0:T(8,128)(2,1)S(1)} collective-permute-done((bf16[264,2048]{1,0:T(8,128)(2,1)}, bf16[264,2048]{1,0:T(8,128)(2,1)S(1)}, u32[]{:S(2)}, u32[]{:S(2)}) %collective-permute-start.3) | collective-permute-done | bytes 1081376 | tf_op jit(solution)/shard_map/ppermute | solution.py:27
  120.3 0.0 copy-start.4
  120.4 0.1 collective-permute-start.6
  120.5 0.0 collective-permute-done.5.refs_1_
  120.5 0.0 copy-start.5
  120.5 2.9 %collective-permute-start.7 = (bf16[128,2048]{1,0:T(8,128)(2,1)S(1)}, bf16[128,2048]{1,0:T(8,128)(2,1)S(1)}, u32[]{:S(2)}, u32[]{:S(2)}) collective-permute-start(bf16[128,2048]{1,0:T(8,128)(2,1)S(1)} %slice.19), channel_id=1, source_target_pairs={{0,131},{1,0},{2,1},{3,2},{128,3},{129,128},{130,129},{131,130},{4... | collective-permute-start | bytes 1572872 | tf_op jit(solution)/shard_map/ppermute | solution.py:27
  123.4 10.4 %collective-permute-done.7.refs_3_ = bf16[128,2048]{1,0:T(8,128)(2,1)S(1)} collective-permute-done((bf16[128,2048]{1,0:T(8,128)(2,1)S(1)}, bf16[128,2048]{1,0:T(8,128)(2,1)S(1)}, u32[]{:S(2)}, u32[]{:S(2)}) %collective-permute-start.7) | collective-permute-done | bytes 524320 | tf_op jit(solution)/shard_map/ppermute | solution.py:27
  133.8 0.0 copy-done.4
  133.8 0.0 copy-done.5
  133.8 0.0 copy-start.8
  133.8 0.8 copy-done.8
  134.6 0.1 collective-permute-done.6.refs_2_
  134.7 0.0 copy-start.7
  134.7 0.8 copy-done.7
  135.5 9.6 %shard_map.50 = bf16[1024,2048]{1,0:T(8,128)(2,1)} custom-call(s32[2]{0:T(128)} %pad_add_fusion.s_ref, bf16[264,2048]{1,0:T(8,128)(2,1)} %copy-done.4, bf16[264,2048]{1,0:T(8,128)(2,1)} %copy-done.5, bf16[136,2048]{1,0:T(8,128)(2,1)} %copy-done.7, bf16[128,2048]{1,0:T(8,128)(2,1)} %copy-done.8), custom_call_target="tpu_custom_call" | custom-call | flops 3221225472 | bytes 7340032 | tf_op jit(solution)/shard_map/pallas_call | solution.py:100
  145.2 0.0 all-to-all-done.3
  145.2 0.0 copy-start
  145.2 1.6 copy-done
  146.7 9.0 %all-to-all-start.2 = ((bf16[32,32,2048]{2,1,0:T(8,128)(2,1)}), bf16[32,32,2048]{2,1,0:T(8,128)(2,1)}, u32[]{:S(2)}, u32[]{:S(2)}) async-start(bf16[32,32,2048]{2,1,0:T(8,128)(2,1)} %bitcast.27), calls=%async_computation.2 | async-start | bytes 8388608 | tf_op jit(solution)/shard_map/all_to_all | solution.py:298
  155.8 1.1 collective-permute-start.8
  156.9 0.7 stack.69.s_ref
  157.6 0.6 stack.79.s_ref
  158.2 1.3 slice.16.a_ref
  159.5 1.2 shard_map.47
  160.7 1.2 slice.17.a_ref
  161.9 1.2 shard_map.49
  163.2 23.1 %collective-permute-done.8.xp_ref = bf16[1280,512]{1,0:T(8,128)(2,1)S(1)} collective-permute-done((bf16[1280,512]{1,0:T(8,128)(2,1)}, bf16[1280,512]{1,0:T(8,128)(2,1)S(1)}, u32[]{:S(2)}, u32[]{:S(2)}) %collective-permute-start.8) | collective-permute-done | bytes 1310752 | tf_op jit(solution)/shard_map/ppermute | solution.py:312
  186.2 0.0 copy-start.6
  186.2 1.1 copy-done.6
  187.3 30.1 %early.1.old_ref = bf16[2048,1024]{1,0:T(8,128)(2,1)} custom-call(s32[9]{0:T(128)} %stack.79.s_ref, bf16[1280,512]{1,0:T(8,128)(2,1)} %bitcast.32, bf16[1280,512]{1,0:T(8,128)(2,1)} %copy-done.6, bf16[1280,512]{1,0:T(8,128)(2,1)} %bitcast.34, bf16[1280,1024]{1,0:T(8,128)(2,1)} %bitcast.28, bf16[1024,2048]{1,0:T(8,128)(2,1)} %bitcast.37), custom_call_target="tpu_custom_call" | custom-call | flops 19327352832 | bytes 18874368 | tf_op jit(solution)/shard_map/early/pallas_call | solution.py:186
  217.4 0.0 all-to-all-done.2
  217.4 15.4 %late.1 = bf16[2048,1024]{1,0:T(8,128)(2,1)} custom-call(s32[6]{0:T(128)} %stack.69.s_ref, bf16[1024,2048]{1,0:T(8,128)(2,1)} %bitcast.13.front_ref.x_ref, bf16[1024,2048]{1,0:T(8,128)(2,1)} %bitcast.13.front_ref.x_ref, bf16[1024,2048]{1,0:T(8,128)(2,1)} %bitcast.38, bf16[2048,1024]{1,0:T(8,128)(2,1)} %early.1.old_ref), custom_call_target="tpu_custom_call", output_to_operand_aliasing={{}: (4, {})} | custom-call | flops 7516192768 | bytes 14680064 | tf_op jit(solution)/shard_map/late/pallas_call | solution.py:241
  (4 shorter events, 0.1 us)
Async XLA Ops:
  11.0 8.7 %copy-start.3 = (bf16[264,2048]{1,0:T(8,128)(2,1)S(1)}, bf16[264,2048]{1,0:T(8,128)(2,1)}, u32[]{:S(2)}) copy-start(bf16[264,2048]{1,0:T(8,128)(2,1)} %pad_maximum_fusion.refs_0_) | copy-start | bytes 3244036
  11.0 47.6 %all-to-all-start = ((bf16[32,40,512]{2,1,0:T(8,128)(2,1)}), bf16[32,40,512]{2,1,0:T(8,128)(2,1)S(1)}, u32[]{:S(2)}, u32[]{:S(2)}) async-start(bf16[32,40,512]{2,1,0:T(8,128)(2,1)} %bitcast.35), calls=%async_computation | async-start | bytes 2621440 | tf_op jit(solution)/shard_map/all_to_all | solution.py:298
  19.7 29.7 %collective-permute-start = (bf16[264,2048]{1,0:T(8,128)(2,1)S(1)}, bf16[264,2048]{1,0:T(8,128)(2,1)}, u32[]{:S(2)}, u32[]{:S(2)}) collective-permute-start(bf16[264,2048]{1,0:T(8,128)(2,1)S(1)} %copy-done.3), channel_id=1, source_target_pairs={{0,1},{1,2},{2,3},{3,128},{128,129},{129,130},{130,131},{131,0},{4... | collective-permute-start | bytes 3244040 | tf_op jit(solution)/shard_map/ppermute | solution.py:27
  21.4 28.1 %collective-permute-start.1 = (bf16[264,2048]{1,0:T(8,128)(2,1)S(1)}, bf16[264,2048]{1,0:T(8,128)(2,1)}, u32[]{:S(2)}, u32[]{:S(2)}) collective-permute-start(bf16[264,2048]{1,0:T(8,128)(2,1)S(1)} %copy-done.3), channel_id=1, source_target_pairs={{0,131},{1,0},{2,1},{3,2},{128,3},{129,128},{130,129},{131,130},{4... | collective-permute-start | bytes 3244040 | tf_op jit(solution)/shard_map/ppermute | solution.py:27
  49.5 26.1 %collective-permute-start.2 = (bf16[264,2048]{1,0:T(8,128)(2,1)}, bf16[264,2048]{1,0:T(8,128)(2,1)}, u32[]{:S(2)}, u32[]{:S(2)}) collective-permute-start(bf16[264,2048]{1,0:T(8,128)(2,1)} %collective-permute-done.refs_0_), channel_id=1, source_target_pairs={{0,1},{1,2},{2,3},{3,128},{128,129},{129,130},{130,131},{131,0},{4... | collective-permute-start | bytes 3244040 | tf_op jit(solution)/shard_map/ppermute | solution.py:27
  49.5 26.1 %collective-permute-start.4 = (bf16[264,2048]{1,0:T(8,128)(2,1)}, bf16[264,2048]{1,0:T(8,128)(2,1)}, u32[]{:S(2)}, u32[]{:S(2)}) collective-permute-start(bf16[264,2048]{1,0:T(8,128)(2,1)} %collective-permute-done.1.refs_1_), channel_id=1, source_target_pairs={{0,131},{1,0},{2,1},{3,2},{128,3},{129,128},{130,129},{131,130},{4... | collective-permute-start | bytes 3244040 | tf_op jit(solution)/shard_map/ppermute | solution.py:27
  58.6 1.1 copy-start.1
  59.7 27.6 %all-to-all-start.1 = ((bf16[32,40,512]{2,1,0:T(8,128)(2,1)}), bf16[32,40,512]{2,1,0:T(8,128)(2,1)S(1)}, u32[]{:S(2)}, u32[]{:S(2)}) async-start(bf16[32,40,512]{2,1,0:T(8,128)(2,1)} %bitcast.36), calls=%async_computation.1 | async-start | bytes 2621440 | tf_op jit(solution)/shard_map/all_to_all | solution.py:298
  87.3 1.1 copy-start.2
  88.4 56.7 %all-to-all-start.3 = ((bf16[32,40,1024]{2,1,0:T(8,128)(2,1)}), bf16[32,40,1024]{2,1,0:T(8,128)(2,1)S(1)}, u32[]{:S(2)}, u32[]{:S(2)}) async-start(bf16[32,40,1024]{2,1,0:T(8,128)(2,1)} %bitcast.29), calls=%async_computation.3 | async-start | bytes 5242880 | tf_op jit(solution)/shard_map/all_to_all | solution.py:298
  93.7 26.6 %collective-permute-start.3 = (bf16[264,2048]{1,0:T(8,128)(2,1)}, bf16[264,2048]{1,0:T(8,128)(2,1)S(1)}, u32[]{:S(2)}, u32[]{:S(2)}) collective-permute-start(bf16[264,2048]{1,0:T(8,128)(2,1)} %collective-permute-done.2.refs_0_), channel_id=1, source_target_pairs={{0,1},{1,2},{2,3},{3,128},{128,129},{129,130},{130,131},{131,0},{4... | collective-permute-start | bytes 3244040 | tf_op jit(solution)/shard_map/ppermute | solution.py:27
  93.8 26.7 %collective-permute-start.5 = (bf16[264,2048]{1,0:T(8,128)(2,1)}, bf16[264,2048]{1,0:T(8,128)(2,1)S(1)}, u32[]{:S(2)}, u32[]{:S(2)}) collective-permute-start(bf16[264,2048]{1,0:T(8,128)(2,1)} %collective-permute-done.4.refs_1_), channel_id=1, source_target_pairs={{0,131},{1,0},{2,1},{3,2},{128,3},{129,128},{130,129},{131,130},{4... | collective-permute-start | bytes 3244040 | tf_op jit(solution)/shard_map/ppermute | solution.py:27
  120.3 13.5 %copy-start.4 = (bf16[264,2048]{1,0:T(8,128)(2,1)}, bf16[264,2048]{1,0:T(8,128)(2,1)S(1)}, u32[]{:S(2)}) copy-start(bf16[264,2048]{1,0:T(8,128)(2,1)S(1)} %collective-permute-done.3.refs_0_) | copy-start | bytes 3244036
  120.4 14.3 %collective-permute-start.6 = (bf16[136,2048]{1,0:T(8,128)(2,1)S(1)}, bf16[136,2048]{1,0:T(8,128)(2,1)S(1)}, u32[]{:S(2)}, u32[]{:S(2)}) collective-permute-start(bf16[136,2048]{1,0:T(8,128)(2,1)S(1)} %slice.18), channel_id=1, source_target_pairs={{0,1},{1,2},{2,3},{3,128},{128,129},{129,130},{130,131},{131,0},{4... | collective-permute-start | bytes 1671176 | tf_op jit(solution)/shard_map/ppermute | solution.py:27
  120.5 13.3 %copy-start.5 = (bf16[264,2048]{1,0:T(8,128)(2,1)}, bf16[264,2048]{1,0:T(8,128)(2,1)S(1)}, u32[]{:S(2)}) copy-start(bf16[264,2048]{1,0:T(8,128)(2,1)S(1)} %collective-permute-done.5.refs_1_) | copy-start | bytes 3244036
  120.5 13.3 %collective-permute-start.7 = (bf16[128,2048]{1,0:T(8,128)(2,1)S(1)}, bf16[128,2048]{1,0:T(8,128)(2,1)S(1)}, u32[]{:S(2)}, u32[]{:S(2)}) collective-permute-start(bf16[128,2048]{1,0:T(8,128)(2,1)S(1)} %slice.19), channel_id=1, source_target_pairs={{0,131},{1,0},{2,1},{3,2},{128,3},{129,128},{130,129},{131,130},{4... | collective-permute-start | bytes 1572872 | tf_op jit(solution)/shard_map/ppermute | solution.py:27
  133.8 0.8 copy-start.8
  134.7 0.8 copy-start.7
  145.2 1.6 copy-start
  146.7 70.7 %all-to-all-start.2 = ((bf16[32,32,2048]{2,1,0:T(8,128)(2,1)}), bf16[32,32,2048]{2,1,0:T(8,128)(2,1)}, u32[]{:S(2)}, u32[]{:S(2)}) async-start(bf16[32,32,2048]{2,1,0:T(8,128)(2,1)} %bitcast.27), calls=%async_computation.2 | async-start | bytes 8388608 | tf_op jit(solution)/shard_map/all_to_all | solution.py:298
  155.8 30.4 %collective-permute-start.8 = (bf16[1280,512]{1,0:T(8,128)(2,1)}, bf16[1280,512]{1,0:T(8,128)(2,1)S(1)}, u32[]{:S(2)}, u32[]{:S(2)}) collective-permute-start(bf16[1280,512]{1,0:T(8,128)(2,1)} %bitcast.30), channel_id=1, source_target_pairs={{0,1},{1,0},{2,3},{3,2},{128,129},{129,128},{130,131},{131,130},{4... | collective-permute-start | bytes 3932168 | tf_op jit(solution)/shard_map/ppermute | solution.py:312
  186.2 1.1 copy-start.6
